TPU v7x, 512 devices: a whole 4x4x16 slice. The times are simulated.
512 devices in a mesh: gx: 64 (over x, z), gy: 8 (over y, core).
Axes of the slice: x: 4, y: 4, z: 16, core: 2. Of those that a mesh axis runs over, the one named last changes fastest.
Arguments:
- u_old: bfloat16 [128, 16, 64, 128], P('gx', 'gy'), may hold values from -6 to 6
- rhs: bfloat16 [128, 16, 64, 128], P('gx', 'gy'), may hold values from -6 to 6
- classes: int32 [128, 16, 16], P('gx', 'gy'), may hold values from 0 to 7
- flags: int32 [2, 128, 16, 16], P(None, 'gx', 'gy'), may hold values from 0 to 1
- inverse: float32 [8, 64, 64], replicated, may hold values from -2 to 2
- x_face: float32 [8, 16, 16], replicated, may hold values from -2 to 2
- lateral_faces: float32 [4, 8, 16, 16], replicated, may hold values from -1.5 to 1.5
- inflow: float32 [16, 16, 128], P('gy'), may hold values from -6 to 6
Outputs:
- u_new: float32 [128, 16, 64, 128], P('gx', 'gy')
All inputs are finite; a program needn't handle non-finite values.
Results may differ from a plain program's by a relative error of at most 0.0003.
Values may be sent and summed in bfloat16 or wider, within the bound.
A program may use at most 64 MiB of HBM per device.

v0:
```python
import jax
import jax.numpy as jnp
from jax import lax
from jax.sharding import PartitionSpec as P

TRACERS = 8
NCLASS = 8
NZ = 16


HIGH = lax.Precision.HIGHEST


def passed_along(value, axis, steps):
    count = lax.axis_size(axis)
    initial, last = (max(0, -steps), min(count, count - steps))
    return lax.ppermute(value, axis, [(source, source + steps) for source in range(initial, last)])


def face_traces(field):
    planes, rows_y, columns = (field.shape[0], field.shape[1], field.shape[3])
    cube = field.reshape(planes, rows_y, 4, 4, 4, columns)
    y_low = cube[:, :, :, 0].reshape(planes, rows_y, 16, columns)
    y_high = cube[:, :, :, 3].reshape(planes, rows_y, 16, columns)
    z_low = cube[:, :, :, :, 0].reshape(planes, rows_y, 16, columns)
    z_high = cube[:, :, :, :, 3].reshape(planes, rows_y, 16, columns)
    return (y_low, y_high, z_low, z_high)


def along_z(trace, upward):
    planes, rows_y, columns = (trace.shape[0], trace.shape[1], trace.shape[3])
    split = trace.reshape(planes, rows_y, 16, TRACERS, NZ)
    border = jnp.zeros((planes, rows_y, 16, TRACERS, 1), trace.dtype)
    if upward:
        moved = jnp.concatenate([border, split[..., :-1]], axis=4)
    else:
        moved = jnp.concatenate([split[..., 1:], border], axis=4)
    return moved.reshape(planes, rows_y, 16, columns)


def class_onehot(classes):
    labels = jnp.arange(NCLASS, dtype=jnp.int32)[:, None, None, None]
    return (classes[None] == labels).astype(jnp.float32)


def class_columns(onehot):
    count, planes, rows_y = (onehot.shape[0], onehot.shape[1], onehot.shape[2])
    spread = jnp.broadcast_to(
        onehot[:, :, :, None, None, :], (count, planes, rows_y, 1, TRACERS, NZ)
    )
    return spread.reshape(count, planes, rows_y, 1, TRACERS * NZ)


def flag_columns(flag):
    planes, rows_y = (flag.shape[0], flag.shape[1])
    spread = jnp.broadcast_to(
        flag.astype(jnp.float32)[:, :, None, None, :], (planes, rows_y, 1, TRACERS, NZ)
    )
    return spread.reshape(planes, rows_y, 1, TRACERS * NZ)


def lateral_rhs(rhs, u_old, below_row, above_row, class_cols, flags, lateral_faces):
    y_low, y_high, z_low, z_high = face_traces(u_old)
    from_below = jnp.concatenate([below_row, y_high[:, :-1]], axis=1).astype(jnp.float32)
    from_above = jnp.concatenate([y_low[:, 1:], above_row], axis=1).astype(jnp.float32)
    from_front = along_z(z_high, True).astype(jnp.float32)
    from_back = along_z(z_low, False).astype(jnp.float32)
    y_flag = flag_columns(flags[0])
    z_flag = flag_columns(flags[1])

    def couple(face_index, source, weight):
        every = jnp.einsum("kij,xyjc->kxyic", lateral_faces[face_index], source, precision=HIGH)
        return jnp.sum(every * class_cols, axis=0) * weight

    planes, rows_y, columns = (rhs.shape[0], rhs.shape[1], rhs.shape[3])
    shape = (planes, rows_y, 4, 4, columns)
    cube = rhs.astype(jnp.float32).reshape(planes, rows_y, 4, 4, 4, columns)
    cube = cube.at[:, :, :, 0].add(-couple(0, from_below, 1.0 - y_flag).reshape(shape))
    cube = cube.at[:, :, :, 3].add(-couple(1, from_above, y_flag).reshape(shape))
    cube = cube.at[:, :, :, :, 0].add(-couple(2, from_front, 1.0 - z_flag).reshape(shape))
    cube = cube.at[:, :, :, :, 3].add(-couple(3, from_back, z_flag).reshape(shape))
    return cube.reshape(planes, rows_y, 64, columns)


def apply_inverse(matrices, source, class_cols):
    total = jnp.zeros(source.shape[:2] + (matrices.shape[1], source.shape[3]), jnp.float32)
    for class_id in range(NCLASS):
        total = total + class_cols[class_id] * jnp.einsum(
            "ij,xyjc->xyic", matrices[class_id], source, precision=HIGH
        )
    return total


def pick(table, hot_plane):
    return jnp.einsum("kab,kyz->yzab", table, hot_plane, precision=HIGH)


def applied(selected, trace):
    return jnp.einsum("...yzab,...ybtz->...yatz", selected, trace, precision=HIGH)


def compose(earlier, later):
    joined = jnp.einsum("...yzab,...yzbc->...yzac", later[0], earlier[0], precision=HIGH)
    return (joined, applied(later[0], earlier[1]) + later[1])


def on_device(u_old, rhs, classes, flags, inverse, x_face, lateral_faces, inflow):
    planes, rows_y, columns = (u_old.shape[0], u_old.shape[1], u_old.shape[3])
    y_low, y_high, z_low, z_high = face_traces(u_old)
    below_row = passed_along(y_high[:, -1:], "gy", 1)
    above_row = passed_along(y_low[:, :1], "gy", -1)
    onehot = class_onehot(classes)
    class_cols = class_columns(onehot)
    source = lateral_rhs(rhs, u_old, below_row, above_row, class_cols, flags, lateral_faces)
    coupling = -jnp.einsum("kij,kjl->kil", inverse[:, :, :16], x_face, precision=HIGH)
    transfer = coupling[:, 48:]
    solved_local = apply_inverse(inverse, source, class_cols)
    outflow_rows = solved_local[:, :, 48:]
    hot_planes = jnp.moveaxis(onehot, 1, 0)
    identity_map = jnp.broadcast_to(jnp.eye(16, dtype=jnp.float32), (rows_y, NZ, 16, 16))
    empty_trace = jnp.zeros((rows_y, 16, TRACERS, NZ), jnp.float32)

    def compose_plane(carry, items):
        outflow, hot_plane = items
        step_map = pick(transfer, hot_plane)
        return (compose(carry, (step_map, outflow)), None)

    outflow_split = outflow_rows.reshape(planes, rows_y, 16, TRACERS, NZ)
    (propagator, offset), _ = lax.scan(
        compose_plane, (identity_map, empty_trace), (outflow_split, hot_planes)
    )
    start = inflow.reshape(rows_y, 16, TRACERS, NZ)
    position = lax.axis_index("gx")
    all_props, all_offsets = (
        lax.all_gather(propagator[None], "gx", axis=0, tiled=True),
        lax.all_gather(offset[None], "gx", axis=0, tiled=True),
    )
    upstream = jnp.arange(all_props.shape[0], dtype=jnp.int32)

    def fold_upstream(carry, items):
        prop_item, offset_item, rank = items
        joined = compose(carry, (prop_item, offset_item))
        keep = rank < position
        return ((jnp.where(keep, joined[0], carry[0]), jnp.where(keep, joined[1], carry[1])), None)

    (chosen_prop, chosen_offset), _ = lax.scan(
        fold_upstream, (identity_map, empty_trace), (all_props, all_offsets, upstream)
    )
    entering = applied(chosen_prop, start) + chosen_offset

    def sweep(trace, items):
        values, hot_plane = items
        result = values.reshape(rows_y, 64, TRACERS, NZ) + applied(pick(coupling, hot_plane), trace)
        return (result[:, 48:], result.reshape(rows_y, 64, columns))

    _, u_new = lax.scan(sweep, entering, (solved_local, hot_planes))
    return u_new


def solution(mesh):
    in_specs = (
        P("gx", "gy", None, None),
        P("gx", "gy", None, None),
        P("gx", "gy", None),
        P(None, "gx", "gy", None),
        P(),
        P(),
        P(),
        P("gy", None, None),
    )
    out_specs = P("gx", "gy", None, None)
    return jax.shard_map(
        on_device, mesh=mesh, in_specs=in_specs, out_specs=out_specs, check_vma=False
    )
```

profile of v0, /device:TPU:6, one launch (start us, length us, event | category | flops | bytes accessed | tf_op | source)
XLA Modules:
  0.0 731.2 jit_solution(3697262948164696308)
XLA Ops:
  7.3 1.7 collective-permute-start
  17.5 1.5 convolution_negate_fusion
  32.0 3.4 while.43
  37.3 160.2 %all-gather.7.cloned.1.call-done = f32[128,16,8,16]{3,2,1,0:T(8,128)} async-done(((f32[2,16,8,16]{3,2,1,0:T(8,128)}), f32[128,16,8,16]{3,2,1,0:T(8,128)}) %all-gather.7.cloned.1.call-update) | async-done | bytes 1048592 | tf_op jit(solution)/shard_map/all_gather | solution.py:136
  197.5 190.8 %all-gather.5.cloned.1.call-done = f32[128,16,16,16]{3,2,1,0:T(8,128)} async-done(((f32[2,16,16,16]{3,2,1,0:T(8,128)}), f32[128,16,16,16]{3,2,1,0:T(8,128)}) %all-gather.5.cloned.1.call-update) | async-done | bytes 2097168 | tf_op jit(solution)/shard_map/all_gather | solution.py:135
  388.4 332.4 %while.44 = (s32[]{:T(128)}, f32[2,16,16,16]{3,2,1,0:T(8,128)S(1)}, f32[2,16,8,16]{1,2,3,0:T(8,128)S(1)}, s32[64]{0:T(128)S(1)}, s32[]{:T(128)}, /*index=5*/f32[...) while((s32[]{:T(128)}, f32[2,16,16,16]{3,2,1,0:T(8,128)S(1)}, ...), condition=%wide.region_7.0_spmd.clone, body=%wide.region_6.0_spmd.clone.sunk | while | flops 2383876 | bytes 1657472 | solution.py:146
  390.7 1.5 fusion.144
  395.9 1.5 fusion.144
  401.1 1.5 fusion.144
  406.3 1.5 fusion.144
  411.5 1.5 fusion.144
  416.7 1.5 fusion.144
  421.8 1.5 fusion.144
  427.0 1.5 fusion.144
  432.2 1.5 fusion.144
  437.4 1.5 fusion.144
  442.6 1.5 fusion.144
  447.8 1.5 fusion.144
  453.0 1.5 fusion.144
  458.2 1.5 fusion.144
  463.4 1.5 fusion.144
  468.6 1.5 fusion.144
  473.8 1.5 fusion.144
  479.0 1.5 fusion.144
  484.2 1.5 fusion.144
  489.4 1.5 fusion.144
  494.6 1.5 fusion.144
  499.7 1.5 fusion.144
  504.9 1.5 fusion.144
  510.1 1.5 fusion.144
  515.3 1.5 fusion.144
  520.5 1.5 fusion.144
  525.7 1.5 fusion.144
  530.9 1.5 fusion.144
  541.3 1.5 fusion.144
  546.5 1.5 fusion.144
  551.7 1.5 fusion.144
  556.9 1.5 fusion.144
  562.1 1.5 fusion.144
  572.5 1.5 fusion.144
  577.6 1.5 fusion.144
  582.8 1.5 fusion.144
  588.0 1.5 fusion.144
  593.2 1.5 fusion.144
  598.4 1.5 fusion.144
  608.8 1.5 fusion.144
  614.0 1.5 fusion.144
  624.4 1.5 fusion.144
  629.6 1.5 fusion.144
  634.8 1.5 fusion.144
  645.2 1.5 fusion.144
  650.4 1.5 fusion.144
  660.7 1.5 fusion.144
  665.9 1.5 fusion.144
  671.1 1.5 fusion.144
  676.3 1.5 fusion.144
  681.5 1.5 fusion.144
  686.7 1.5 fusion.144
  697.1 1.5 fusion.144
  702.3 1.5 fusion.144
  707.5 1.5 fusion.144
  712.7 1.5 fusion.144
  717.9 1.5 fusion.144
  721.3 2.5 while.42
  (513 shorter events, 232.4 us)
Async XLA Ops:
  6.5 10.9 %copy-start = (f32[8,16,16]{2,1,0:T(8,128)S(1)}, f32[8,16,16]{2,1,0:T(8,128)}, u32[]{:S(2)}) copy-start(f32[8,16,16]{2,1,0:T(8,128)} %param.27) | copy-start | bytes 24580
  6.5 30.5 %copy-start.2 = (f32[2,16,128]{2,1,0:T(8,128)S(1)}, f32[2,16,128]{2,1,0:T(8,128)}, u32[]{:S(2)}) copy-start(f32[2,16,128]{2,1,0:T(8,128)} %param.29) | copy-start | bytes 49156
  6.5 191.0 %all-gather.7.cloned.1.call-start = ((), (), s32[]{:S(2)}) async-start(), calls=%async_computation.1 | async-start | bytes 8519680 | tf_op jit(solution)/shard_map/all_gather | solution.py:136
  7.3 13.4 %collective-permute-start = (bf16[2,1,16,128]{3,2,1,0:T(8,128)(2,1)S(1)}, bf16[2,1,16,128]{3,2,1,0:T(8,128)(2,1)S(1)}, u32[]{:S(2)}, u32[]{:S(2)}) collective-permute-start(bf16[2,1,16,128]{3,2,1,0:T(8,128)(2,1)S(1)} %get-tuple-element.301), channel_id=1, source_target_pairs={{0,1},{1,2},{2,3},{3,4},{4,5},{5,6},{6,7},{8,9},{9,10},{10,11},{11... | collective-permute-start | bytes 24584 | tf_op jit(solution)/shard_map/ppermute | solution.py:17
  9.1 12.8 %collective-permute-start.1 = (bf16[2,1,16,128]{3,2,1,0:T(8,128)(2,1)S(1)}, bf16[2,1,16,128]{3,2,1,0:T(8,128)(2,1)S(1)}, u32[]{:S(2)}, u32[]{:S(2)}) collective-permute-start(bf16[2,1,16,128]{3,2,1,0:T(8,128)(2,1)S(1)} %get-tuple-element.300), channel_id=1, source_target_pairs={{1,0},{2,1},{3,2},{4,3},{5,4},{6,5},{7,6},{9,8},{10,9},{11,10},{12... | collective-permute-start | bytes 24584 | tf_op jit(solution)/shard_map/ppermute | solution.py:17
  35.5 0.9 copy-start.1
  36.3 352.1 %all-gather.5.cloned.1.call-start = ((), (), s32[]{:S(2)}) async-start(), calls=%async_computation | async-start | bytes 17039360 | tf_op jit(solution)/shard_map/all_gather | solution.py:135
  723.7 0.7 copy-start.3
Sparse Core Ops, SparseCore 0:
  36.4 161.0 all-gather.6
  200.5 187.8 all-gather.4
where the time goes:
time: 740 us; the launch traced here: 731 us
  waiting for transfers between devices  352 us (48%)
  matrix products  200 us (27%)
  local copies, waits for them, and re-layouts  113 us (15%)
  loops' own time  45.8 us (6%)
  between operations  13.8 us (2%)
    all_gather x1, waiting for transfers between devices, on_device(): lax.all_gather(propagator[None], 'gx', axis=0, tiled=True)  191 us
    all_gather x1, waiting for transfers between devices, on_device(): lax.all_gather(offset[None], 'gx', axis=0, tiled=True)  160 us
    dynamic_slice x192, local copies, waits for them, and re-layouts, on_device(): lax.scan(fold_upstream, (identity_map, empty_trace), (all_props, all_offs...  104 us
    dot_general x69, matrix products, applied(): jnp.einsum('...yzab,...ybtz->...yatz', selected, trace, precision=HIGH)  98 us
    dot_general x66, matrix products, compose(): jnp.einsum('...yzab,...yzbc->...yzac', later[0], earlier[0], precision=HIGH)  86.6 us
    another operation x1, loops' own time, on_device(): lax.scan(fold_upstream, (identity_map, empty_trace), (all_props, all_offs...  45.5 us
  transfers between devices with their start and end apart: 4, of which 2 were waited for; matrix products, arithmetic and copies ran while one was open for 2% of the time, Pallas kernels for 0%

commit v1 on v0

v1 whole, which is shorter than its diff:
```python
import functools

import jax
import jax.numpy as jnp
from jax import lax
from jax.experimental import pallas as pl
from jax.experimental.pallas import tpu as pltpu
from jax.sharding import PartitionSpec as P

MESH = pl.DeviceIdType.MESH
NCLASS = 8
NZ = 16
LANES = 128
F32 = jnp.float32
BF16 = jnp.bfloat16
HIGHEST = lax.Precision.HIGHEST


def gather_plan(ring):
    far = {16: (6, -6, 3, -3), 8: (3, -3)}.get(ring, ())
    steps = (1, -1) if ring > 2 else (1,)
    covered = {0} | {f % ring for f in far}
    relays = []
    for held in (0,) + tuple(f % ring for f in far[::-1]):
        for step in steps:
            target = (held + step) % ring
            if target not in covered:
                covered.add(target)
                relays.append((held, step))
    for held in (0,) + tuple(f % ring for f in far):
        for step in (2, -2):
            target = (held + step) % ring
            if target not in covered:
                covered.add(target)
                relays.append((held, step))
    assert covered == set(range(ring)), covered
    return far, relays


def iota(shape, axis):
    return lax.broadcasted_iota(jnp.int32, shape, axis)


def lanes_of(value, index):
    return jnp.take_along_axis(value, index, axis=1, mode="promise_in_bounds")


def spread(ref, row):
    return jnp.broadcast_to(ref[pl.ds(row, 1), :], (8, LANES))


def total_of(terms):
    while len(terms) > 1:
        terms = [sum(terms[i : i + 2]) for i in range(0, len(terms), 2)]
    return terms[0]


def high_low(value):
    high = value.astype(BF16)
    return high, (value - high.astype(F32)).astype(BF16)


def pick_class(stacked, rows, masks):
    result = stacked[0:rows]
    for k in range(1, NCLASS):
        result = jnp.where(masks[k], stacked[k * rows : (k + 1) * rows], result)
    return result


def kernel(
    xd, zd, yd,
    u_hbm, rhs_hbm, cls_hbm, flg_hbm, inv_hbm, xf_hbm, lat_hbm, inflow_hbm,
    out_ref,
    u_v, rhs_v, cls_v, flg_v, inv_v, xf_v, lat_v, inflow_v, halo,
    meta_in, meta, ih, il, mhl, tw, src, rh, wo,
    clsb, ob, tmp, ec, up, vp, px, xo, ex, xp, ent, tr1,
    local_sem, halo_ss, halo_rs, cls_ss, cls_rs, o_ss, o_rs, px_ss, px_rs, xo_ss, xo_rs,
):
    gx, gy = lax.axis_index("gx"), lax.axis_index("gy")
    x, z = gx // zd, lax.rem(gx, zd)

    def at(dx=0, dz=0, dy=0):
        gx_to = lax.rem(x + dx + xd, xd) * zd + lax.rem(z + dz + zd, zd)
        return (gx_to, lax.rem(gy + dy + yd, yd))

    far, relays = gather_plan(zd)
    barrier = pltpu.get_barrier_semaphore()
    peers = [at(dz=d) for d in range(1, zd)] + [at(dx=d) for d in range(1, xd)] + [at(dy=1), at(dy=-1)]
    for peer in peers:
        pl.semaphore_signal(barrier, inc=1, device_id=peer, device_id_type=MESH)

    loads = [
        pltpu.make_async_copy(a, b, local_sem.at[i])
        for i, (a, b) in enumerate(
            [(inv_hbm, inv_v), (lat_hbm, lat_v), (xf_hbm, xf_v), (cls_hbm, cls_v), (flg_hbm, flg_v), (u_hbm, u_v), (rhs_hbm, rhs_v), (inflow_hbm, inflow_v)]
        )
    ]
    for load in loads:
        load.start()

    meta_in[...] = jnp.zeros_like(meta_in)
    loads[3].wait()
    loads[4].wait()
    for p in range(2):
        for r in range(2):
            meta_in[pl.ds(p * 2 + r, 1), pl.ds(0, NZ)] = cls_v[p, pl.ds(r, 1), :].astype(F32)
            for f in range(2):
                meta_in[pl.ds(4 + f * 4 + p * 2 + r, 1), pl.ds(0, NZ)] = flg_v[f, p, pl.ds(r, 1), :].astype(F32)
    row, col = iota((LANES, LANES), 0), iota((LANES, LANES), 1)
    tile = ((row < NZ) & (row == (col & 15))).astype(BF16)
    meta[...] = jnp.dot(meta_in[...].astype(BF16), tile, preferred_element_type=F32)
    clsb[0] = jnp.concatenate([meta[pl.ds(0, 4), :] * 16.0, jnp.zeros((4, LANES), F32)], axis=0)

    loads[0].wait()
    loads[1].wait()
    loads[2].wait()
    inv_all = inv_v[...].reshape(NCLASS * 64, 64)
    ih_value, il_value = high_low(inv_all)
    ih[...] = ih_value.reshape(NCLASS, 64, 64)
    il[...] = il_value.reshape(NCLASS, 64, 64)
    node, slot = iota((64, LANES), 0), iota((64, LANES), 1)
    face, j = slot >> 4, slot & 15
    a, b = j >> 2, j & 3
    y_node = 16 * a + b
    wanted = jnp.where(face == 0, y_node, jnp.where(face == 1, y_node + 12, jnp.where(face == 2, 4 * j, jnp.where(face == 3, 4 * j + 3, jnp.where(face == 4, j, -1)))))
    faces_of = jnp.dot(inv_all, (node == wanted).astype(F32), precision=HIGHEST, preferred_element_type=F32)
    tables = jnp.concatenate([lat_v[...].reshape(4 * NCLASS * 16, 16), xf_v[...].reshape(NCLASS * 16, 16)], axis=0)
    source_slot, sj = iota((16, LANES), 1), iota((16, LANES), 0)

    def slot_face_and_j(s):
        y_face = jnp.where((s & 7) < 4, 1, 0)
        y_j = 4 * (s >> 3) + (s & 3)
        t = s - 32
        z_face = jnp.where((t & 3) == 3, 2, jnp.where((t & 3) == 0, 3, -1))
        z_j = t >> 2
        in_face = jnp.where(s < 32, y_face, jnp.where(s < 96, z_face, 4))
        in_j = jnp.where(s < 32, y_j, jnp.where(s < 96, z_j, s & 15))
        return in_face, in_j

    _, column_j = slot_face_and_j(source_slot)
    placed = jnp.dot(tables, (column_j == sj).astype(F32), precision=HIGHEST, preferred_element_type=F32)
    slot_face, _ = slot_face_and_j(iota((16, LANES), 1))
    lane16 = iota((16, LANES), 1)
    tw_value = jnp.zeros((16, LANES), F32)
    for k in range(NCLASS):
        blocks = []
        for f in range(5):
            start = (f * NCLASS + k) * 16
            blocks.append(jnp.where(slot_face == f, placed[start : start + 16], 0.0))
        blocks.append(jnp.zeros((48, LANES), F32))
        matrix = -jnp.dot(faces_of[k * 64 : (k + 1) * 64], jnp.concatenate(blocks, axis=0), precision=HIGHEST, preferred_element_type=F32)
        high, low = high_low(matrix)
        mhl[k, :, pl.ds(0, LANES)] = high
        mhl[k, :, pl.ds(LANES, LANES)] = low
        kept = jnp.where((lane16 >= 96) & (lane16 < 112), matrix[48:64], 0.0)
        tw_value = tw_value + pltpu.roll(kept, (16 * k - 96) % LANES, 1)
    tw[...] = tw_value

    loads[5].wait()
    loads[6].wait()
    loads[7].wait()
    pl.semaphore_wait(barrier, len(peers))

    cls_copies = [
        pltpu.make_async_remote_copy(clsb.at[0], clsb.at[d], cls_ss.at[d - 1], cls_rs.at[d - 1], device_id=at(dz=d), device_id_type=MESH)
        for d in range(1, zd)
    ]
    halo_copies = [
        pltpu.make_async_remote_copy(u_v.at[:, 1], halo.at[0], halo_ss.at[0], halo_rs.at[0], device_id=at(dy=1), device_id_type=MESH),
        pltpu.make_async_remote_copy(u_v.at[:, 0], halo.at[1], halo_ss.at[1], halo_rs.at[1], device_id=at(dy=-1), device_id_type=MESH),
    ]
    for copy in halo_copies + cls_copies:
        copy.start()

    lane64, node64 = iota((64, LANES), 1), iota((64, LANES), 0)
    lane_z = lane64 & 15
    node_c = node64 & 3
    for p in range(2):
        for r in range(2):
            columns = pl.ds(r * LANES, LANES)
            rh[p, :, columns] = rhs_v[p, r]
            own = u_v[p, r].astype(F32)
            z_flag = meta[pl.ds(8 + p * 2 + r, 1), :]
            front = jnp.where(lane_z > 0, pltpu.roll(own, 1, 1), 0.0) * (1.0 - z_flag)
            back = jnp.where(lane_z < 15, pltpu.roll(own, LANES - 1, 1), 0.0) * z_flag
            z_source = jnp.where(node_c == 3, front, jnp.where(node_c == 0, back, 0.0))
            src[p, pl.ds(32, 64), columns] = z_source.astype(BF16)
            src[p, pl.ds(96, 32), columns] = jnp.zeros((32, LANES), BF16)
    for copy in halo_copies:
        copy.wait()
    has_below = jnp.where(gy > 0, 1.0, 0.0)
    has_above = jnp.where(gy < yd - 1, 1.0, 0.0)
    sub8 = iota((8, LANES), 0)
    for p in range(2):
        for r in range(2):
            y_flag = meta[pl.ds(4 + p * 2 + r, 1), :]
            if r == 0:
                below, above = halo[0, p].astype(F32), u_v[p, 1].astype(F32)
                m_below, m_above = (1.0 - y_flag) * has_below, y_flag
            else:
                below, above = u_v[p, 0].astype(F32), halo[1, p].astype(F32)
                m_below, m_above = 1.0 - y_flag, y_flag * has_above
            pieces = []
            for a_ in range(4):
                pieces.append(jnp.where(sub8 < 4, above[16 * a_ : 16 * a_ + 8] * m_above, below[16 * a_ + 8 : 16 * a_ + 16] * m_below))
            src[p, pl.ds(0, 32), pl.ds(r * LANES, LANES)] = jnp.concatenate(pieces, axis=0).astype(BF16)

    inv_high_out = ih[:, 48:64, :].reshape(NCLASS * 16, 64)
    inv_low_out = il[:, 48:64, :].reshape(NCLASS * 16, 64)
    lat_out = mhl[:, 48:64, :].reshape(NCLASS * 16, 2 * LANES)

    def class_masks(p, r, rows):
        labels = jnp.broadcast_to(meta[pl.ds(p * 2 + r, 1), :], (rows, LANES))
        return [labels == float(k) for k in range(NCLASS)]

    for p in range(2):
        source = src[p]
        stacked = (
            jnp.dot(lat_out, jnp.concatenate([source, source], axis=0), preferred_element_type=F32)
            + jnp.dot(inv_high_out, rh[p], preferred_element_type=F32)
            + jnp.dot(inv_low_out, rh[p], preferred_element_type=F32)
        )
        for r in range(2):
            wo[p, r] = pick_class(stacked[:, r * LANES : (r + 1) * LANES], 16, class_masks(p, r, 16))

    def class_step(index_row, source_ref):
        base = jnp.broadcast_to(clsb[0, pl.ds(index_row, 1), :], (8, LANES)).astype(jnp.int32)
        low, high = [], []
        for m in range(16):
            value = spread(source_ref, m)
            low.append(lanes_of(tw[pl.ds(0, 8), :], base + m) * value)
            high.append(lanes_of(tw[pl.ds(8, 8), :], base + m) * value)
        return total_of(low), total_of(high)

    for r in range(2):
        low, high = class_step(2 + r, wo.at[0, r])
        ob[0, r, pl.ds(0, 8), :] = low + wo[1, r, pl.ds(0, 8), :]
        ob[0, r, pl.ds(8, 8), :] = high + wo[1, r, pl.ds(8, 8), :]

    def o_copy(held, step):
        to = (held + step) % zd
        return pltpu.make_async_remote_copy(ob.at[held], ob.at[to], o_ss.at[to - 1], o_rs.at[to - 1], device_id=at(dz=step), device_id_type=MESH)

    started = {}

    def send(held, step):
        copy = o_copy(held, step)
        copy.start()
        started[(held + step) % zd] = copy

    for f in far:
        send(0, f)
    for held, step in relays:
        if held == 0:
            send(0, step)

    def relay(offset):
        started[offset % zd].wait_recv()
        for held, step in relays:
            if held == offset % zd:
                send(held, step)

    for copy in cls_copies:
        copy.wait()
    lane8 = iota((8, LANES), 1)
    lane_unit, lane_low = lane8 >> 4, lane8 & 15

    def propagator(d, carry):
        for r in range(2):
            first = jnp.broadcast_to(clsb[d, pl.ds(r, 1), :], (8, LANES)).astype(jnp.int32) + lane_unit
            second = jnp.broadcast_to(clsb[d, pl.ds(2 + r, 1), :], (8, LANES)).astype(jnp.int32)
            for h in range(2):
                for half in range(2):
                    tmp[r, h, pl.ds(half * 8, 8), :] = lanes_of(tw[pl.ds(half * 8, 8), :], first + 8 * h)
            sums = [[[] for _ in range(2)] for _ in range(2)]
            for m in range(16):
                values = [spread(tmp.at[r, h], m) for h in range(2)]
                for half in range(2):
                    factor = lanes_of(tw[pl.ds(half * 8, 8), :], second + m)
                    for h in range(2):
                        sums[h][half].append(factor * values[h])
            for h in range(2):
                for half in range(2):
                    whole = total_of(sums[h][half])
                    for unit in range(8):
                        ec[d, r, 8 * h + unit, pl.ds(half * 8, 8), :] = lanes_of(whole, lane_low + 16 * unit)
        return carry

    def propagators(start, stop):
        lax.fori_loop(start, stop, propagator, 0)

    def unit_step(i, carry):
        d = lax.rem(z - i + zd, zd)
        for r in range(2):
            sums = [[[] for _ in range(2)] for _ in range(2)]
            for m in range(16):
                values = [spread(up.at[i, r, h], m) for h in range(2)]
                for half in range(2):
                    factor = ec[d, r, m, pl.ds(half * 8, 8), :]
                    for h in range(2):
                        sums[h][half].append(factor * values[h])
            for h in range(2):
                for half in range(2):
                    up[i + 1, r, h, pl.ds(half * 8, 8), :] = total_of(sums[h][half])
        return carry

    def full_planes(p, carry):
        source = src[p]
        both = jnp.concatenate([source, source], axis=0)
        stacked = (
            jnp.dot(mhl[...].reshape(NCLASS * 64, 2 * LANES), both, preferred_element_type=F32)
            + jnp.dot(ih[...].reshape(NCLASS * 64, 64), rh[p], preferred_element_type=F32)
            + jnp.dot(il[...].reshape(NCLASS * 64, 64), rh[p], preferred_element_type=F32)
        )
        for r in range(2):
            labels = jnp.broadcast_to(meta[pl.ds(p * 2 + r, 1), :], (64, LANES))
            out_ref[p, r] = pick_class(stacked[:, r * LANES : (r + 1) * LANES], 64, [labels == float(k) for k in range(NCLASS)])
        return carry

    propagators(0, zd)
    for f in far[::-1]:
        relay(f)
    for r in range(2):
        for h in range(2):
            units = iota((16, LANES), 1) >> 4
            up[0, r, h] = (iota((16, LANES), 0) == units + 8 * h).astype(F32)
    lax.fori_loop(0, zd, unit_step, 0)
    px_copies = [
        pltpu.make_async_remote_copy(up.at[zd], px.at[d - 1], px_ss.at[d - 1], px_rs.at[d - 1], device_id=at(dx=d), device_id_type=MESH)
        for d in range(1, xd)
    ]
    for copy in px_copies:
        copy.start()
    lax.fori_loop(0, 2, full_planes, 0)

    def expand(value_ref, slot):
        for r in range(2):
            for h in range(2):
                for half in range(2):
                    whole = value_ref[r, h, pl.ds(half * 8, 8), :]
                    for unit in range(8):
                        ex[slot, r, 8 * h + unit, pl.ds(half * 8, 8), :] = lanes_of(whole, lane_low + 16 * unit)

    expand(up.at[z], xd - 1)
    for copy in px_copies:
        copy.wait()

    def expand_slot(d, carry):
        expand(px.at[d], d)
        return carry

    lax.fori_loop(0, xd - 1, expand_slot, 0)

    def apply(factors, source, r):
        low, high = [], []
        for m in range(16):
            value = spread(source, m)
            low.append(factors[m, pl.ds(0, 8), :] * value)
            high.append(factors[m, pl.ds(8, 8), :] * value)
        return total_of(low), total_of(high)

    for d in range(1, zd):
        if d not in [f % zd for f in far]:
            started[d].wait_recv()
    vp[0] = jnp.zeros((2, 16, LANES), F32)

    def group_step(i, carry):
        d = lax.rem(z - i + zd, zd)
        for r in range(2):
            low, high = apply(ec.at[d, r], vp.at[i, r], r)
            vp[i + 1, r, pl.ds(0, 8), :] = low + ob[d, r, pl.ds(0, 8), :]
            vp[i + 1, r, pl.ds(8, 8), :] = high + ob[d, r, pl.ds(8, 8), :]
        return carry

    lax.fori_loop(0, zd, group_step, 0)
    xo_copies = [
        pltpu.make_async_remote_copy(vp.at[zd], xo.at[d - 1], xo_ss.at[d - 1], xo_rs.at[d - 1], device_id=at(dx=d), device_id_type=MESH)
        for d in range(1, xd)
    ]
    for copy in xo_copies:
        copy.start()
    xp[0] = inflow_v[...]
    for copy in xo_copies:
        copy.wait()

    def x_step(i, carry):
        d = x - i - 1
        for r in range(2):
            low, high = apply(ex.at[d, r], xp.at[i, r], r)
            xp[i + 1, r, pl.ds(0, 8), :] = low + xo[d, r, pl.ds(0, 8), :]
            xp[i + 1, r, pl.ds(8, 8), :] = high + xo[d, r, pl.ds(8, 8), :]
        return carry

    lax.fori_loop(0, x, x_step, 0)
    for r in range(2):
        low, high = apply(ex.at[xd - 1, r], xp.at[x, r], r)
        ent[r, pl.ds(0, 8), :] = low + vp[z, r, pl.ds(0, 8), :]
        ent[r, pl.ds(8, 8), :] = high + vp[z, r, pl.ds(8, 8), :]
    for r in range(2):
        low, high = class_step(r, ent.at[r])
        tr1[r, pl.ds(0, 8), :] = low + wo[0, r, pl.ds(0, 8), :]
        tr1[r, pl.ds(8, 8), :] = high + wo[0, r, pl.ds(8, 8), :]

    for p, trace in enumerate((ent, tr1)):
        high, low = high_low(jnp.concatenate([trace[0], trace[1]], axis=1))
        half = jnp.concatenate([jnp.zeros((96, 2 * LANES), BF16), high, low], axis=0)
        stacked = jnp.dot(mhl[...].reshape(NCLASS * 64, 2 * LANES), jnp.concatenate([half, half], axis=0), preferred_element_type=F32)
        for r in range(2):
            out_ref[p, r] = out_ref[p, r] + pick_class(stacked[:, r * LANES : (r + 1) * LANES], 64, class_masks(p, r, 64))

    for copy in started.values():
        copy.wait_send()


def solution(mesh):
    gxs, yd = mesh.shape["gx"], mesh.shape["gy"]
    zd = min(16, gxs // 2)
    xd = gxs // zd

    def on_device(u_old, rhs, classes, flags, inverse, x_face, lateral_faces, inflow):
        any_space = pl.BlockSpec(memory_space=pl.ANY)
        dma = pltpu.SemaphoreType.DMA
        return pl.pallas_call(
            functools.partial(kernel, xd, zd, yd),
            name="sweep",
            out_shape=jax.ShapeDtypeStruct((2, 2, 64, LANES), F32),
            in_specs=[any_space] * 8,
            out_specs=pl.BlockSpec(memory_space=pltpu.VMEM),
            scratch_shapes=[
                pltpu.VMEM((2, 2, 64, LANES), BF16),
                pltpu.VMEM((2, 2, 64, LANES), BF16),
                pltpu.VMEM((2, 2, NZ), jnp.int32),
                pltpu.VMEM((2, 2, 2, NZ), jnp.int32),
                pltpu.VMEM((NCLASS, 64, 64), F32),
                pltpu.VMEM((NCLASS, 16, 16), F32),
                pltpu.VMEM((4, NCLASS, 16, 16), F32),
                pltpu.VMEM((2, 16, LANES), F32),
                pltpu.VMEM((2, 2, 64, LANES), BF16),
                pltpu.VMEM((16, LANES), F32),
                pltpu.VMEM((16, LANES), F32),
                pltpu.VMEM((NCLASS, 64, 64), BF16),
                pltpu.VMEM((NCLASS, 64, 64), BF16),
                pltpu.VMEM((NCLASS, 64, 2 * LANES), BF16),
                pltpu.VMEM((16, LANES), F32),
                pltpu.VMEM((2, LANES, 2 * LANES), BF16),
                pltpu.VMEM((2, 64, 2 * LANES), BF16),
                pltpu.VMEM((2, 2, 16, LANES), F32),
                pltpu.VMEM((zd, 8, LANES), F32),
                pltpu.VMEM((zd, 2, 16, LANES), F32),
                pltpu.VMEM((2, 2, 16, LANES), F32),
                pltpu.VMEM((zd, 2, 16, 16, LANES), F32),
                pltpu.VMEM((zd + 1, 2, 2, 16, LANES), F32),
                pltpu.VMEM((zd + 1, 2, 16, LANES), F32),
                pltpu.VMEM((xd - 1, 2, 2, 16, LANES), F32),
                pltpu.VMEM((xd - 1, 2, 16, LANES), F32),
                pltpu.VMEM((xd, 2, 16, 16, LANES), F32),
                pltpu.VMEM((xd, 2, 16, LANES), F32),
                pltpu.VMEM((2, 16, LANES), F32),
                pltpu.VMEM((2, 16, LANES), F32),
                dma((8,)),
                dma((2,)),
                dma((2,)),
                dma((zd - 1,)),
                dma((zd - 1,)),
                dma((zd - 1,)),
                dma((zd - 1,)),
                dma((xd - 1,)),
                dma((xd - 1,)),
                dma((xd - 1,)),
                dma((xd - 1,)),
            ],
            compiler_params=pltpu.CompilerParams(collective_id=0, has_side_effects=True),
        )(u_old, rhs, classes, flags, inverse, x_face, lateral_faces, inflow)

    return jax.shard_map(
        on_device,
        mesh=mesh,
        in_specs=(
            P("gx", "gy", None, None),
            P("gx", "gy", None, None),
            P("gx", "gy", None),
            P(None, "gx", "gy", None),
            P(),
            P(),
            P(),
            P("gy", None, None),
        ),
        out_specs=P("gx", "gy", None, None),
        check_vma=False,
    )
```

time: 740 us -> 43.9 us (0.06)
  the two profiles are of different devices: /device:TPU:6 before, /device:TPU:24 now
where the time goes in v1:
time: 43.9 us; the launch traced here: 43.8 us
  Pallas kernels  42.2 us (96%)
  local copies, waits for them, and re-layouts  1.57 us (4%)
    pallas_call x1, Pallas kernels, on_device(): pl.pallas_call(functools.partial(kernel, xd, zd, yd), name='sweep', out_s...  42.2 us
    unnamed x1, local copies, waits for them, and re-layouts  1.57 us

profile of v1, /device:TPU:24, one launch (start us, length us, event | category | flops | bytes accessed | tf_op | source)
XLA Modules:
  0.0 43.8 jit_solution(10361200371076246964)
XLA Ops:
  0.0 42.2 %sweep.1 = f32[2,2,64,128]{3,2,1,0:T(8,128)} custom-call(bf16[2,2,64,128]{3,2,1,0:T(8,128)(2,1)} %u_hbm.1, bf16[2,2,64,128]{3,2,1,0:T(8,128)(2,1)} %rhs_hbm.1, s32[2,2,16]{2,1,0:T(2,128)} %cls_hbm.1, s32[2,2,2,16]{3,2,1,0:T(2,128)} %flg_hbm.1, f32[8,64,64]{2,1,0:T(8,128)} %inv_hbm.1, f32[8,16,16]{2,1,0:T(8,128)} %xf_hbm.1, f32[4,8,16,16]{3,2,1,0:T(8,128)} %lat_hbm.1, ...), custom_call_target="tpu_custom_call" | custom-call | tf_op jit(solution)/shard_map/sweep/pallas_call | solution.py:423
  42.2 1.6 %copy.10 = f32[2,2,64,128]{3,2,1,0:T(8,128)} copy(f32[2,2,64,128]{3,2,1,0:T(8,128)} %sweep.1) | data formatting | bytes 262144

commit v2 on v1

v2 whole, which is shorter than its diff:
```python
import functools

import jax
import jax.numpy as jnp
from jax import lax
from jax.experimental import pallas as pl
from jax.experimental.pallas import tpu as pltpu
from jax.sharding import PartitionSpec as P

MESH = pl.DeviceIdType.MESH
NCLASS = 8
NZ = 16
LANES = 128
F32 = jnp.float32
BF16 = jnp.bfloat16
HIGHEST = lax.Precision.HIGHEST


def gather_plan(ring):
    assert ring == 16
    far = (5, -5)
    near = (2, -2, 1, -1)
    own = [(0, step) for step in near]
    relays = {5: [(5, 3)] + [(5, step) for step in near], 11: [(11, step) for step in near]}
    covered = {0, 5, 11} | {(held + step) % ring for held, step in own + relays[5] + relays[11]}
    assert covered == set(range(ring)), covered
    return far, own, relays


def iota(shape, axis):
    return lax.broadcasted_iota(jnp.int32, shape, axis)


def lanes_of(value, index):
    return jnp.take_along_axis(value, index, axis=1, mode="promise_in_bounds")


def spread(ref, row):
    return jnp.broadcast_to(ref[pl.ds(row, 1), :], (8, LANES))


def total_of(terms):
    while len(terms) > 1:
        terms = [sum(terms[i : i + 2]) for i in range(0, len(terms), 2)]
    return terms[0]


def high_low(value):
    high = value.astype(BF16)
    return high, (value - high.astype(F32)).astype(BF16)


def pick_class(stacked, rows, masks):
    result = stacked[0:rows]
    for k in range(1, NCLASS):
        result = jnp.where(masks[k], stacked[k * rows : (k + 1) * rows], result)
    return result


def kernel(
    xd, zd, yd,
    u_hbm, rhs_hbm, cls_hbm, flg_hbm, inv_hbm, xf_hbm, lat_hbm, inflow_hbm,
    out_ref,
    u_v, rhs_v, cls_v, flg_v, inv_v, xf_v, lat_v, inflow_v, halo,
    meta_in, meta, ih, il, mhl, tw, c1s, t0s, pairs, src, rh, wo,
    clsb, ob, ec, up, vp, px, xo, ex, xp, ent, tr1,
    local_sem, halo_ss, halo_rs, cls_ss, cls_rs, o_ss, o_rs, px_ss, px_rs, xo_ss, xo_rs,
):
    gx, gy = lax.axis_index("gx"), lax.axis_index("gy")
    x, z = gx // zd, lax.rem(gx, zd)

    def at(dx=0, dz=0, dy=0):
        gx_to = lax.rem(x + dx + xd, xd) * zd + lax.rem(z + dz + zd, zd)
        return (gx_to, lax.rem(gy + dy + yd, yd))

    loads = [
        pltpu.make_async_copy(a, b, local_sem.at[i])
        for i, (a, b) in enumerate(
            [(cls_hbm, cls_v), (flg_hbm, flg_v), (u_hbm, u_v), (inv_hbm, inv_v), (lat_hbm, lat_v), (xf_hbm, xf_v), (rhs_hbm, rhs_v), (inflow_hbm, inflow_v)]
        )
    ]
    for load in loads:
        load.start()
    far, own_near, relays = gather_plan(zd)
    barrier = pltpu.get_barrier_semaphore()
    peers = [at(dy=1), at(dy=-1)] + [at(dz=d) for d in (1, -1, 2, -2, 3, -3, 5, -5)] + [at(dx=d) for d in range(1, xd)]
    for peer in peers:
        pl.semaphore_signal(barrier, inc=1, device_id=peer, device_id_type=MESH)

    meta_in[...] = jnp.zeros_like(meta_in)
    loads[0].wait()
    loads[1].wait()
    for p in range(2):
        for r in range(2):
            meta_in[pl.ds(p * 2 + r, 1), pl.ds(0, NZ)] = cls_v[p, pl.ds(r, 1), :].astype(F32)
            for f in range(2):
                meta_in[pl.ds(4 + f * 4 + p * 2 + r, 1), pl.ds(0, NZ)] = flg_v[f, p, pl.ds(r, 1), :].astype(F32)
    row, col = iota((LANES, LANES), 0), iota((LANES, LANES), 1)
    tile = ((row < NZ) & (row == (col & 15))).astype(BF16)
    meta_value = jnp.dot(meta_in[...].astype(BF16), tile, preferred_element_type=F32)
    meta[...] = meta_value
    pair = meta_value[0:2] * 8.0 + meta_value[2:4]
    clsb[0] = jnp.where(iota((1, LANES), 1) < NZ, pair[0:1], pair[1:2])

    loads[3].wait()
    loads[4].wait()
    loads[5].wait()
    inv_all = inv_v[...].reshape(NCLASS * 64, 64)
    ih_value, il_value = high_low(inv_all)
    ih[...] = ih_value.reshape(NCLASS, 64, 64)
    il[...] = il_value.reshape(NCLASS, 64, 64)
    node, slot = iota((64, LANES), 0), iota((64, LANES), 1)
    face, j = slot >> 4, slot & 15
    a, b = j >> 2, j & 3
    y_node = 16 * a + b
    wanted = jnp.where(face == 0, y_node, jnp.where(face == 1, y_node + 12, jnp.where(face == 2, 4 * j, jnp.where(face == 3, 4 * j + 3, jnp.where(face == 4, j, -1)))))
    faces_of = jnp.dot(inv_all, (node == wanted).astype(F32), precision=HIGHEST, preferred_element_type=F32)
    tables = jnp.concatenate([lat_v[...].reshape(4 * NCLASS * 16, 16), xf_v[...].reshape(NCLASS * 16, 16)], axis=0)
    source_slot, sj = iota((16, LANES), 1), iota((16, LANES), 0)

    def slot_face_and_j(s):
        y_face = jnp.where((s & 7) < 4, 1, 0)
        y_j = 4 * (s >> 3) + (s & 3)
        t = s - 32
        z_face = jnp.where((t & 3) == 3, 2, jnp.where((t & 3) == 0, 3, -1))
        z_j = t >> 2
        in_face = jnp.where(s < 32, y_face, jnp.where(s < 96, z_face, 4))
        in_j = jnp.where(s < 32, y_j, jnp.where(s < 96, z_j, s & 15))
        return in_face, in_j

    slot_face, column_j = slot_face_and_j(source_slot)
    placed = jnp.dot(tables, (column_j == sj).astype(F32), precision=HIGHEST, preferred_element_type=F32)
    tw_value = jnp.zeros((16, LANES), F32)
    for k in range(NCLASS):
        blocks = []
        for f in range(5):
            start = (f * NCLASS + k) * 16
            blocks.append(jnp.where(slot_face == f, placed[start : start + 16], 0.0))
        blocks.append(jnp.zeros((48, LANES), F32))
        matrix = -jnp.dot(faces_of[k * 64 : (k + 1) * 64], jnp.concatenate(blocks, axis=0), precision=HIGHEST, preferred_element_type=F32)
        high, low = high_low(matrix)
        mhl[k, :, pl.ds(0, LANES)] = high
        mhl[k, :, pl.ds(LANES, LANES)] = low
        kept = jnp.where((source_slot >= 96) & (source_slot < 112), matrix[48:64], 0.0)
        tw_value = tw_value + pltpu.roll(kept, (16 * k - 96) % LANES, 1)
    tw[...] = tw_value
    halves = [pl.ds(0, 8), pl.ds(8, 8)]

    loads[2].wait()
    loads[6].wait()
    loads[7].wait()
    lane64, node64 = iota((64, LANES), 1), iota((64, LANES), 0)
    lane_z = lane64 & 15
    node_c = node64 & 3
    for p in range(2):
        for r in range(2):
            columns = pl.ds(r * LANES, LANES)
            rh[p, :, columns] = rhs_v[p, r]
            own = u_v[p, r].astype(F32)
            z_flag = meta[pl.ds(8 + p * 2 + r, 1), :]
            front = jnp.where(lane_z > 0, pltpu.roll(own, 1, 1), 0.0) * (1.0 - z_flag)
            back = jnp.where(lane_z < 15, pltpu.roll(own, LANES - 1, 1), 0.0) * z_flag
            z_source = jnp.where(node_c == 3, front, jnp.where(node_c == 0, back, 0.0))
            src[p, pl.ds(32, 64), columns] = z_source.astype(BF16)
            src[p, pl.ds(96, 32), columns] = jnp.zeros((32, LANES), BF16)

    pl.semaphore_wait(barrier, len(peers))

    halo_copies = [
        pltpu.make_async_remote_copy(u_v.at[:, 1], halo.at[0], halo_ss.at[0], halo_rs.at[0], device_id=at(dy=1), device_id_type=MESH),
        pltpu.make_async_remote_copy(u_v.at[:, 0], halo.at[1], halo_ss.at[1], halo_rs.at[1], device_id=at(dy=-1), device_id_type=MESH),
    ]
    for copy in halo_copies:
        copy.start()

    def sender(buffer, send_sems, recv_sems):
        copies = {}

        def send(held, step):
            to = (held + step) % zd
            copies[to] = pltpu.make_async_remote_copy(buffer.at[held], buffer.at[to], send_sems.at[to - 1], recv_sems.at[to - 1], device_id=at(dz=step), device_id_type=MESH)
            copies[to].start()

        return copies, send

    cls_copies, send_cls = sender(clsb, cls_ss, cls_rs)
    o_copies, send_o = sender(ob, o_ss, o_rs)

    def send_own(send):
        for step in far:
            send(0, step)
        for held, step in own_near:
            send(held, step)

    def relay(copies, send, offset):
        copies[offset].wait_recv()
        for held, step in relays[offset]:
            send(held, step)

    send_own(send_cls)

    lane8 = iota((8, LANES), 1)
    pair_first, pair_second = ((lane8 >> 3) & 7) * 16, (lane8 & 7) * 16
    for m in range(16):
        for half in range(2):
            c1s[m, halves[half], :] = lanes_of(tw[halves[half], :], pair_second + m)
            t0s[m, halves[half], :] = lanes_of(tw[halves[half], :], pair_first + m)
    lane16 = iota((16, LANES), 1)

    def pair_product(jj, carry):
        sums = [[], []]
        for m in range(16):
            value = spread(t0s.at[jj], m)
            for half in range(2):
                sums[half].append(c1s[m, halves[half], :] * value)
        product = jnp.concatenate([total_of(sums[0]), total_of(sums[1])], axis=0)
        high = product.astype(BF16)
        rest = product - high.astype(F32)
        middle = rest.astype(BF16)
        low = (rest - middle.astype(F32)).astype(BF16)
        pairs[jj, :, pl.ds(0, LANES)] = jnp.where(lane16 < 64, high.astype(F32), middle.astype(F32)).astype(BF16)
        pairs[jj, :, pl.ds(LANES, LANES)] = jnp.where(lane16 < 64, low.astype(F32), 0.0).astype(BF16)
        return carry

    lax.fori_loop(0, 16, pair_product, 0)

    for copy in halo_copies:
        copy.wait()

    has_below = jnp.where(gy > 0, 1.0, 0.0)
    has_above = jnp.where(gy < yd - 1, 1.0, 0.0)
    sub8 = iota((8, LANES), 0)
    for p in range(2):
        for r in range(2):
            y_flag = meta[pl.ds(4 + p * 2 + r, 1), :]
            if r == 0:
                below, above = halo[0, p].astype(F32), u_v[p, 1].astype(F32)
                m_below, m_above = (1.0 - y_flag) * has_below, y_flag
            else:
                below, above = u_v[p, 0].astype(F32), halo[1, p].astype(F32)
                m_below, m_above = 1.0 - y_flag, y_flag * has_above
            pieces = []
            for a_ in range(4):
                pieces.append(jnp.where(sub8 < 4, above[16 * a_ : 16 * a_ + 8] * m_above, below[16 * a_ + 8 : 16 * a_ + 16] * m_below))
            src[p, pl.ds(0, 32), pl.ds(r * LANES, LANES)] = jnp.concatenate(pieces, axis=0).astype(BF16)

    inv_high_out = ih[:, 48:64, :].reshape(NCLASS * 16, 64)
    inv_low_out = il[:, 48:64, :].reshape(NCLASS * 16, 64)
    lat_out = mhl[:, 48:64, :].reshape(NCLASS * 16, 2 * LANES)

    def class_masks(p, r, rows):
        labels = jnp.broadcast_to(meta[pl.ds(p * 2 + r, 1), :], (rows, LANES))
        return [labels == float(k) for k in range(NCLASS)]

    for p in range(2):
        source = src[p]
        stacked = (
            jnp.dot(lat_out, jnp.concatenate([source, source], axis=0), preferred_element_type=F32)
            + jnp.dot(inv_high_out, rh[p], preferred_element_type=F32)
            + jnp.dot(inv_low_out, rh[p], preferred_element_type=F32)
        )
        for r in range(2):
            wo[p, r] = pick_class(stacked[:, r * LANES : (r + 1) * LANES], 16, class_masks(p, r, 16))

    def class_step(index_row, source_ref):
        base = (jnp.broadcast_to(meta[pl.ds(index_row, 1), :], (8, LANES)) * 16.0).astype(jnp.int32)
        sums = [[], []]
        for m in range(16):
            value = spread(source_ref, m)
            for half in range(2):
                sums[half].append(lanes_of(tw[halves[half], :], base + m) * value)
        return total_of(sums[0]), total_of(sums[1])

    for r in range(2):
        parts = class_step(2 + r, wo.at[0, r])
        for half in range(2):
            ob[0, r, halves[half], :] = parts[half] + wo[1, r, halves[half], :]

    send_own(send_o)
    for offset in relays:
        relay(cls_copies, send_cls, offset)

    def full_planes(p, carry):
        source = src[p]
        both = jnp.concatenate([source, source], axis=0)
        stacked = (
            jnp.dot(mhl[...].reshape(NCLASS * 64, 2 * LANES), both, preferred_element_type=F32)
            + jnp.dot(ih[...].reshape(NCLASS * 64, 64), rh[p], preferred_element_type=F32)
            + jnp.dot(il[...].reshape(NCLASS * 64, 64), rh[p], preferred_element_type=F32)
        )
        for r in range(2):
            labels = jnp.broadcast_to(meta[pl.ds(p * 2 + r, 1), :], (64, LANES))
            out_ref[p, r] = pick_class(stacked[:, r * LANES : (r + 1) * LANES], 64, [labels == float(k) for k in range(NCLASS)])
        return carry

    lax.fori_loop(0, 2, full_planes, 0)

    pair_rows = iota((64, LANES), 0)
    lane_low = lane8 & 15

    def propagators(slots):
        for d in slots:
            if d > 0 and d not in relays:
                cls_copies[d].wait_recv()
            hot = []
            for r in range(2):
                labels = lanes_of(jnp.broadcast_to(clsb[d], (8, LANES)), lane_low + 16 * r)
                hot.append((jnp.concatenate([labels] * 8, axis=0).astype(jnp.int32) == pair_rows).astype(F32).astype(BF16))
            one = jnp.concatenate(hot, axis=1)
            every = jnp.dot(pairs[...].reshape(256, 2 * LANES), jnp.concatenate([one, one, one, one], axis=0), preferred_element_type=F32)
            for r in range(2):
                ec[d, r] = every[:, r * LANES : (r + 1) * LANES].reshape(16, 16, LANES)

    propagators((0, 1, 15, 2, 14, 5, 11))
    for offset in relays:
        relay(o_copies, send_o, offset)
    propagators((4, 12, 6, 10, 3, 13, 7, 9, 8))

    def unit_step(i, carry):
        d = lax.rem(z - i + zd, zd)
        for r in range(2):
            sums = [[[] for _ in range(2)] for _ in range(2)]
            for m in range(16):
                values = [spread(up.at[i, r, h], m) for h in range(2)]
                for half in range(2):
                    factor = ec[d, r, m, halves[half], :]
                    for h in range(2):
                        sums[h][half].append(factor * values[h])
            for h in range(2):
                for half in range(2):
                    up[i + 1, r, h, halves[half], :] = total_of(sums[h][half])
        return carry

    for r in range(2):
        for h in range(2):
            up[0, r, h] = (iota((16, LANES), 0) == (lane16 >> 4) + 8 * h).astype(F32)
    lax.fori_loop(0, zd, unit_step, 0)

    px_copies = [
        pltpu.make_async_remote_copy(up.at[zd], px.at[d - 1], px_ss.at[d - 1], px_rs.at[d - 1], device_id=at(dx=d), device_id_type=MESH)
        for d in range(1, xd)
    ]
    for copy in px_copies:
        copy.start()

    def expand(value_ref, slot):
        for r in range(2):
            for h in range(2):
                for half in range(2):
                    whole = value_ref[r, h, halves[half], :]
                    for unit in range(8):
                        ex[slot, r, 8 * h + unit, halves[half], :] = lanes_of(whole, lane_low + 16 * unit)

    expand(up.at[z], xd - 1)

    def apply(factors, source):
        sums = [[], []]
        for m in range(16):
            value = spread(source, m)
            for half in range(2):
                sums[half].append(factors[m, halves[half], :] * value)
        return total_of(sums[0]), total_of(sums[1])

    for d in range(1, zd):
        if d not in relays:
            o_copies[d].wait_recv()
    vp[0] = jnp.zeros((2, 16, LANES), F32)

    def group_step(i, carry):
        d = lax.rem(z - i + zd, zd)
        for r in range(2):
            parts = apply(ec.at[d, r], vp.at[i, r])
            for half in range(2):
                vp[i + 1, r, halves[half], :] = parts[half] + ob[d, r, halves[half], :]
        return carry

    lax.fori_loop(0, zd, group_step, 0)
    xo_copies = [
        pltpu.make_async_remote_copy(vp.at[zd], xo.at[d - 1], xo_ss.at[d - 1], xo_rs.at[d - 1], device_id=at(dx=d), device_id_type=MESH)
        for d in range(1, xd)
    ]
    for copy in xo_copies:
        copy.start()
    for copy in px_copies:
        copy.wait()

    def expand_slot(d, carry):
        expand(px.at[d], d)
        return carry

    lax.fori_loop(0, xd - 1, expand_slot, 0)
    xp[0] = inflow_v[...]
    for copy in xo_copies:
        copy.wait()

    def x_step(i, carry):
        d = x - i - 1
        for r in range(2):
            parts = apply(ex.at[d, r], xp.at[i, r])
            for half in range(2):
                xp[i + 1, r, halves[half], :] = parts[half] + xo[d, r, halves[half], :]
        return carry

    lax.fori_loop(0, x, x_step, 0)
    for r in range(2):
        parts = apply(ex.at[xd - 1, r], xp.at[x, r])
        for half in range(2):
            ent[r, halves[half], :] = parts[half] + vp[z, r, halves[half], :]
    for r in range(2):
        parts = class_step(r, ent.at[r])
        for half in range(2):
            tr1[r, halves[half], :] = parts[half] + wo[0, r, halves[half], :]

    for p, trace in enumerate((ent, tr1)):
        high, low = high_low(jnp.concatenate([trace[0], trace[1]], axis=1))
        half_rows = jnp.concatenate([jnp.zeros((96, 2 * LANES), BF16), high, low], axis=0)
        stacked = jnp.dot(mhl[...].reshape(NCLASS * 64, 2 * LANES), jnp.concatenate([half_rows, half_rows], axis=0), preferred_element_type=F32)
        for r in range(2):
            out_ref[p, r] = out_ref[p, r] + pick_class(stacked[:, r * LANES : (r + 1) * LANES], 64, class_masks(p, r, 64))

    for copy in list(cls_copies.values()) + list(o_copies.values()):
        copy.wait_send()


def solution(mesh):
    gxs, yd = mesh.shape["gx"], mesh.shape["gy"]
    zd = min(16, gxs // 2)
    xd = gxs // zd

    def on_device(u_old, rhs, classes, flags, inverse, x_face, lateral_faces, inflow):
        any_space = pl.BlockSpec(memory_space=pl.ANY)
        dma = pltpu.SemaphoreType.DMA
        return pl.pallas_call(
            functools.partial(kernel, xd, zd, yd),
            name="sweep",
            out_shape=pltpu.VMEM((2, 2, 64, LANES), F32),
            in_specs=[any_space] * 8,
            out_specs=pl.BlockSpec(memory_space=pltpu.VMEM),
            scratch_shapes=[
                pltpu.VMEM((2, 2, 64, LANES), BF16),
                pltpu.VMEM((2, 2, 64, LANES), BF16),
                pltpu.VMEM((2, 2, NZ), jnp.int32),
                pltpu.VMEM((2, 2, 2, NZ), jnp.int32),
                pltpu.VMEM((NCLASS, 64, 64), F32),
                pltpu.VMEM((NCLASS, 16, 16), F32),
                pltpu.VMEM((4, NCLASS, 16, 16), F32),
                pltpu.VMEM((2, 16, LANES), F32),
                pltpu.VMEM((2, 2, 64, LANES), BF16),
                pltpu.VMEM((16, LANES), F32),
                pltpu.VMEM((16, LANES), F32),
                pltpu.VMEM((NCLASS, 64, 64), BF16),
                pltpu.VMEM((NCLASS, 64, 64), BF16),
                pltpu.VMEM((NCLASS, 64, 2 * LANES), BF16),
                pltpu.VMEM((16, LANES), F32),
                pltpu.VMEM((16, 16, LANES), F32),
                pltpu.VMEM((16, 16, LANES), F32),
                pltpu.VMEM((16, 16, 2 * LANES), BF16),
                pltpu.VMEM((2, LANES, 2 * LANES), BF16),
                pltpu.VMEM((2, 64, 2 * LANES), BF16),
                pltpu.VMEM((2, 2, 16, LANES), F32),
                pltpu.VMEM((zd, 1, LANES), F32),
                pltpu.VMEM((zd, 2, 16, LANES), F32),
                pltpu.VMEM((zd, 2, 16, 16, LANES), F32),
                pltpu.VMEM((zd + 1, 2, 2, 16, LANES), F32),
                pltpu.VMEM((zd + 1, 2, 16, LANES), F32),
                pltpu.VMEM((xd - 1, 2, 2, 16, LANES), F32),
                pltpu.VMEM((xd - 1, 2, 16, LANES), F32),
                pltpu.VMEM((xd, 2, 16, 16, LANES), F32),
                pltpu.VMEM((xd, 2, 16, LANES), F32),
                pltpu.VMEM((2, 16, LANES), F32),
                pltpu.VMEM((2, 16, LANES), F32),
                dma((8,)),
                dma((2,)),
                dma((2,)),
                dma((zd - 1,)),
                dma((zd - 1,)),
                dma((zd - 1,)),
                dma((zd - 1,)),
                dma((xd - 1,)),
                dma((xd - 1,)),
                dma((xd - 1,)),
                dma((xd - 1,)),
            ],
            compiler_params=pltpu.CompilerParams(collective_id=0, has_side_effects=True),
        )(u_old, rhs, classes, flags, inverse, x_face, lateral_faces, inflow)

    return jax.shard_map(
        on_device,
        mesh=mesh,
        in_specs=(
            P("gx", "gy", None, None),
            P("gx", "gy", None, None),
            P("gx", "gy", None),
            P(None, "gx", "gy", None),
            P(),
            P(),
            P(),
            P("gy", None, None),
        ),
        out_specs=P("gx", "gy", None, None),
        check_vma=False,
    )
```

time: 43.9 us -> 33.9 us (0.77)
  the two profiles are of different devices: /device:TPU:24 before, /device:TPU:8 now
where the time goes in v2:
time: 33.9 us; the launch traced here: 33.7 us
  Pallas kernels  33.1 us (98%)
  local copies, waits for them, and re-layouts  0.66 us (2%)
    pallas_call x1, Pallas kernels, on_device(): pl.pallas_call(functools.partial(kernel, xd, zd, yd), name='sweep', out_s...  33.1 us

profile of v2, /device:TPU:8, one launch (start us, length us, event | category | flops | bytes accessed | tf_op | source)
XLA Modules:
  0.0 33.7 jit_solution(11781957288222788896)
XLA Ops:
  0.0 33.1 %sweep.1 = f32[2,2,64,128]{3,2,1,0:T(8,128)S(1)} custom-call(bf16[2,2,64,128]{3,2,1,0:T(8,128)(2,1)} %u_hbm.1, bf16[2,2,64,128]{3,2,1,0:T(8,128)(2,1)} %rhs_hbm.1, s32[2,2,16]{2,1,0:T(2,128)} %cls_hbm.1, s32[2,2,2,16]{3,2,1,0:T(2,128)} %flg_hbm.1, f32[8,64,64]{2,1,0:T(8,128)} %inv_hbm.1, f32[8,16,16]{2,1,0:T(8,128)} %xf_hbm.1, f32[4,8,16,16]{3,2,1,0:T(8,128)} %lat_hbm.1, ...), custom_call_target="tpu_custom_call" | custom-call | tf_op jit(solution)/shard_map/sweep/pallas_call | solution.py:433
  33.1 0.7 %copy.10 = f32[2,2,64,128]{3,2,1,0:T(8,128)} copy(f32[2,2,64,128]{3,2,1,0:T(8,128)S(1)} %sweep.1) | data formatting | bytes 262144

commit v3 on v2

--- a/solution.py
+++ b/solution.py
@@ -61,10 +61,10 @@
     xd, zd, yd,
     u_hbm, rhs_hbm, cls_hbm, flg_hbm, inv_hbm, xf_hbm, lat_hbm, inflow_hbm,
     out_ref,
-    u_v, rhs_v, cls_v, flg_v, inv_v, xf_v, lat_v, inflow_v, halo,
+    u_v, rhs_v, cls_v, flg_v, inv_v, xf_v, lat_v, inflow_v, border, halo,
     meta_in, meta, ih, il, mhl, tw, c1s, t0s, pairs, src, rh, wo,
     clsb, ob, ec, up, vp, px, xo, ex, xp, ent, tr1,
-    local_sem, halo_ss, halo_rs, cls_ss, cls_rs, o_ss, o_rs, px_ss, px_rs, xo_ss, xo_rs,
+    know, know_x, local_sem, halo_ss, halo_rs, cls_ss, cls_rs, o_ss, o_rs, px_ss, px_rs, xo_ss, xo_rs,
 ):
     gx, gy = lax.axis_index("gx"), lax.axis_index("gy")
     x, z = gx // zd, lax.rem(gx, zd)
@@ -83,9 +83,22 @@
         load.start()
     far, own_near, relays = gather_plan(zd)
     barrier = pltpu.get_barrier_semaphore()
-    peers = [at(dy=1), at(dy=-1)] + [at(dz=d) for d in (1, -1, 2, -2, 3, -3, 5, -5)] + [at(dx=d) for d in range(1, xd)]
-    for peer in peers:
+    for peer in (at(dy=1), at(dy=-1)) + tuple(at(dz=d) for d in (1, -1, 2, -2, 3, -3)):
         pl.semaphore_signal(barrier, inc=1, device_id=peer, device_id_type=MESH)
+
+    @pl.when(x > 0)
+    def _():
+        pl.semaphore_signal(barrier, inc=1, device_id=at(dx=-1), device_id_type=MESH)
+
+    @pl.when(x < xd - 1)
+    def _():
+        pl.semaphore_signal(barrier, inc=1, device_id=at(dx=1), device_id_type=MESH)
+
+    greeted = 8 + jnp.where(x > 0, 1, 0) + jnp.where(x < xd - 1, 1, 0)
+
+    def tell(semaphore, step):
+        for sign in (1, -1):
+            pl.semaphore_signal(semaphore, inc=1, device_id=at(dz=sign * step), device_id_type=MESH)
 
     meta_in[...] = jnp.zeros_like(meta_in)
     loads[0].wait()
@@ -101,6 +114,58 @@
     meta[...] = meta_value
     pair = meta_value[0:2] * 8.0 + meta_value[2:4]
     clsb[0] = jnp.where(iota((1, LANES), 1) < NZ, pair[0:1], pair[1:2])
+
+    loads[2].wait()
+    sub8 = iota((8, LANES), 0)
+    top = [u_v[p, 1].astype(F32) for p in range(2)]
+    bottom = [u_v[p, 0].astype(F32) for p in range(2)]
+    packed_top, packed_bottom = [], []
+    for a_ in range(4):
+        low_rows, high_rows = slice(16 * a_, 16 * a_ + 8), slice(16 * a_ + 8, 16 * a_ + 16)
+        packed_top.append(jnp.where(sub8 < 4, pltpu.roll(top[0][high_rows], 4, 0), top[1][high_rows]))
+        packed_bottom.append(jnp.where(sub8 < 4, bottom[0][low_rows], pltpu.roll(bottom[1][low_rows], 4, 0)))
+    border[0] = jnp.concatenate(packed_top, axis=0).astype(BF16)
+    border[1] = jnp.concatenate(packed_bottom, axis=0).astype(BF16)
+    pl.semaphore_wait(barrier, greeted)
+
+    halo_copies = [
+        pltpu.make_async_remote_copy(border.at[0], halo.at[0], halo_ss.at[0], halo_rs.at[0], device_id=at(dy=1), device_id_type=MESH),
+        pltpu.make_async_remote_copy(border.at[1], halo.at[1], halo_ss.at[1], halo_rs.at[1], device_id=at(dy=-1), device_id_type=MESH),
+    ]
+    for copy in halo_copies:
+        copy.start()
+    tell(know.at[0], 2)
+
+    @pl.when((x > 0) & (x < xd - 1))
+    def _():
+        pl.semaphore_signal(know_x.at[0], inc=1, device_id=at(dx=-1), device_id_type=MESH)
+
+    def sender(buffer, send_sems, recv_sems):
+        copies = {}
+
+        def send(held, step):
+            to = (held + step) % zd
+            copies[to] = pltpu.make_async_remote_copy(buffer.at[held], buffer.at[to], send_sems.at[to - 1], recv_sems.at[to - 1], device_id=at(dz=step), device_id_type=MESH)
+            copies[to].start()
+
+        return copies, send
+
+    cls_copies, send_cls = sender(clsb, cls_ss, cls_rs)
+    o_copies, send_o = sender(ob, o_ss, o_rs)
+
+    def send_own(send):
+        for step in far:
+            send(0, step)
+        for held, step in own_near:
+            send(held, step)
+
+    for held, step in own_near:
+        send_cls(held, step)
+
+    def relay(copies, send, offset):
+        copies[offset].wait_recv()
+        for held, step in relays[offset]:
+            send(held, step)
 
     loads[3].wait()
     loads[4].wait()
@@ -146,7 +211,6 @@
     tw[...] = tw_value
     halves = [pl.ds(0, 8), pl.ds(8, 8)]
 
-    loads[2].wait()
     loads[6].wait()
     loads[7].wait()
     lane64, node64 = iota((64, LANES), 1), iota((64, LANES), 0)
@@ -164,40 +228,74 @@
             src[p, pl.ds(32, 64), columns] = z_source.astype(BF16)
             src[p, pl.ds(96, 32), columns] = jnp.zeros((32, LANES), BF16)
 
-    pl.semaphore_wait(barrier, len(peers))
-
-    halo_copies = [
-        pltpu.make_async_remote_copy(u_v.at[:, 1], halo.at[0], halo_ss.at[0], halo_rs.at[0], device_id=at(dy=1), device_id_type=MESH),
-        pltpu.make_async_remote_copy(u_v.at[:, 0], halo.at[1], halo_ss.at[1], halo_rs.at[1], device_id=at(dy=-1), device_id_type=MESH),
-    ]
+    for d in (1, 2, zd - 1, zd - 2):
+        cls_copies[d].wait_recv()
+    pl.semaphore_wait(know.at[0], 2)
+    for held in (0, 1, zd - 1, 2, zd - 2):
+        for step in far:
+            send_cls(held, step)
+
     for copy in halo_copies:
-        copy.start()
-
-    def sender(buffer, send_sems, recv_sems):
-        copies = {}
-
-        def send(held, step):
-            to = (held + step) % zd
-            copies[to] = pltpu.make_async_remote_copy(buffer.at[held], buffer.at[to], send_sems.at[to - 1], recv_sems.at[to - 1], device_id=at(dz=step), device_id_type=MESH)
-            copies[to].start()
-
-        return copies, send
-
-    cls_copies, send_cls = sender(clsb, cls_ss, cls_rs)
-    o_copies, send_o = sender(ob, o_ss, o_rs)
-
-    def send_own(send):
-        for step in far:
-            send(0, step)
-        for held, step in own_near:
-            send(held, step)
-
-    def relay(copies, send, offset):
-        copies[offset].wait_recv()
-        for held, step in relays[offset]:
-            send(held, step)
-
-    send_own(send_cls)
+        copy.wait()
+
+    has_below = jnp.where(gy > 0, 1.0, 0.0)
+    has_above = jnp.where(gy < yd - 1, 1.0, 0.0)
+    got_below, got_above = halo[0].astype(F32), halo[1].astype(F32)
+    for p in range(2):
+        for r in range(2):
+            y_flag = meta[pl.ds(4 + p * 2 + r, 1), :]
+            m_below, m_above = 1.0 - y_flag, y_flag
+            if r == 0:
+                m_below = m_below * has_below
+                other = u_v[p, 1].astype(F32)
+            else:
+                m_above = m_above * has_above
+                other = u_v[p, 0].astype(F32)
+            pieces = []
+            for a_ in range(4):
+                tile_rows = slice(8 * a_, 8 * a_ + 8)
+                if r == 0:
+                    below = pltpu.roll(got_below[tile_rows], 4, 0) if p == 0 else got_below[tile_rows]
+                    above = other[16 * a_ : 16 * a_ + 8]
+                else:
+                    below = other[16 * a_ + 8 : 16 * a_ + 16]
+                    above = got_above[tile_rows] if p == 0 else pltpu.roll(got_above[tile_rows], 4, 0)
+                pieces.append(jnp.where(sub8 < 4, above * m_above, below * m_below))
+            src[p, pl.ds(0, 32), pl.ds(r * LANES, LANES)] = jnp.concatenate(pieces, axis=0).astype(BF16)
+
+    inv_high_out = ih[:, 48:64, :].reshape(NCLASS * 16, 64)
+    inv_low_out = il[:, 48:64, :].reshape(NCLASS * 16, 64)
+    lat_out = mhl[:, 48:64, :].reshape(NCLASS * 16, 2 * LANES)
+
+    def class_masks(p, r, rows):
+        labels = jnp.broadcast_to(meta[pl.ds(p * 2 + r, 1), :], (rows, LANES))
+        return [labels == float(k) for k in range(NCLASS)]
+
+    for p in range(2):
+        source = src[p]
+        stacked = (
+            jnp.dot(lat_out, jnp.concatenate([source, source], axis=0), preferred_element_type=F32)
+            + jnp.dot(inv_high_out, rh[p], preferred_element_type=F32)
+            + jnp.dot(inv_low_out, rh[p], preferred_element_type=F32)
+        )
+        for r in range(2):
+            wo[p, r] = pick_class(stacked[:, r * LANES : (r + 1) * LANES], 16, class_masks(p, r, 16))
+
+    def class_step(index_row, source_ref):
+        base = (jnp.broadcast_to(meta[pl.ds(index_row, 1), :], (8, LANES)) * 16.0).astype(jnp.int32)
+        sums = [[], []]
+        for m in range(16):
+            value = spread(source_ref, m)
+            for half in range(2):
+                sums[half].append(lanes_of(tw[halves[half], :], base + m) * value)
+        return total_of(sums[0]), total_of(sums[1])
+
+    for r in range(2):
+        parts = class_step(2 + r, wo.at[0, r])
+        for half in range(2):
+            ob[0, r, halves[half], :] = parts[half] + wo[1, r, halves[half], :]
+
+    send_own(send_o)
 
     lane8 = iota((8, LANES), 1)
     pair_first, pair_second = ((lane8 >> 3) & 7) * 16, (lane8 & 7) * 16
@@ -224,61 +322,17 @@
 
     lax.fori_loop(0, 16, pair_product, 0)
 
-    for copy in halo_copies:
-        copy.wait()
-
-    has_below = jnp.where(gy > 0, 1.0, 0.0)
-    has_above = jnp.where(gy < yd - 1, 1.0, 0.0)
-    sub8 = iota((8, LANES), 0)
-    for p in range(2):
-        for r in range(2):
-            y_flag = meta[pl.ds(4 + p * 2 + r, 1), :]
-            if r == 0:
-                below, above = halo[0, p].astype(F32), u_v[p, 1].astype(F32)
-                m_below, m_above = (1.0 - y_flag) * has_below, y_flag
-            else:
-                below, above = u_v[p, 0].astype(F32), halo[1, p].astype(F32)
-                m_below, m_above = 1.0 - y_flag, y_flag * has_above
-            pieces = []
-            for a_ in range(4):
-                pieces.append(jnp.where(sub8 < 4, above[16 * a_ : 16 * a_ + 8] * m_above, below[16 * a_ + 8 : 16 * a_ + 16] * m_below))
-            src[p, pl.ds(0, 32), pl.ds(r * LANES, LANES)] = jnp.concatenate(pieces, axis=0).astype(BF16)
-
-    inv_high_out = ih[:, 48:64, :].reshape(NCLASS * 16, 64)
-    inv_low_out = il[:, 48:64, :].reshape(NCLASS * 16, 64)
-    lat_out = mhl[:, 48:64, :].reshape(NCLASS * 16, 2 * LANES)
-
-    def class_masks(p, r, rows):
-        labels = jnp.broadcast_to(meta[pl.ds(p * 2 + r, 1), :], (rows, LANES))
-        return [labels == float(k) for k in range(NCLASS)]
-
-    for p in range(2):
-        source = src[p]
-        stacked = (
-            jnp.dot(lat_out, jnp.concatenate([source, source], axis=0), preferred_element_type=F32)
-            + jnp.dot(inv_high_out, rh[p], preferred_element_type=F32)
-            + jnp.dot(inv_low_out, rh[p], preferred_element_type=F32)
-        )
-        for r in range(2):
-            wo[p, r] = pick_class(stacked[:, r * LANES : (r + 1) * LANES], 16, class_masks(p, r, 16))
-
-    def class_step(index_row, source_ref):
-        base = (jnp.broadcast_to(meta[pl.ds(index_row, 1), :], (8, LANES)) * 16.0).astype(jnp.int32)
-        sums = [[], []]
-        for m in range(16):
-            value = spread(source_ref, m)
-            for half in range(2):
-                sums[half].append(lanes_of(tw[halves[half], :], base + m) * value)
-        return total_of(sums[0]), total_of(sums[1])
-
-    for r in range(2):
-        parts = class_step(2 + r, wo.at[0, r])
-        for half in range(2):
-            ob[0, r, halves[half], :] = parts[half] + wo[1, r, halves[half], :]
-
-    send_own(send_o)
-    for offset in relays:
-        relay(cls_copies, send_cls, offset)
+    @pl.when(x < xd - 2)
+    def _():
+        pl.semaphore_wait(know_x.at[0], 1)
+
+    @pl.when((x > 0) & (x < xd - 2))
+    def _():
+        pl.semaphore_signal(know_x.at[1], inc=1, device_id=at(dx=-1), device_id_type=MESH)
+
+    @pl.when(x < xd - 3)
+    def _():
+        pl.semaphore_wait(know_x.at[1], 1)
 
     def full_planes(p, carry):
         source = src[p]
@@ -300,8 +354,6 @@
 
     def propagators(slots):
         for d in slots:
-            if d > 0 and d not in relays:
-                cls_copies[d].wait_recv()
             hot = []
             for r in range(2):
                 labels = lanes_of(jnp.broadcast_to(clsb[d], (8, LANES)), lane_low + 16 * r)
@@ -311,10 +363,17 @@
             for r in range(2):
                 ec[d, r] = every[:, r * LANES : (r + 1) * LANES].reshape(16, 16, LANES)
 
-    propagators((0, 1, 15, 2, 14, 5, 11))
+    propagators((0, 1, 15, 2, 14))
+    middle = (7, 3, 13, 5, 11, 4, 12, 6, 10, 9)
+    for d in middle:
+        cls_copies[d].wait_recv()
+        if d == 7:
+            send_cls(7, 1)
     for offset in relays:
         relay(o_copies, send_o, offset)
-    propagators((4, 12, 6, 10, 3, 13, 7, 9, 8))
+    propagators(middle)
+    cls_copies[8].wait_recv()
+    propagators((8,))
 
     def unit_step(i, carry):
         d = lax.rem(z - i + zd, zd)
@@ -340,8 +399,12 @@
         pltpu.make_async_remote_copy(up.at[zd], px.at[d - 1], px_ss.at[d - 1], px_rs.at[d - 1], device_id=at(dx=d), device_id_type=MESH)
         for d in range(1, xd)
     ]
-    for copy in px_copies:
-        copy.start()
+    for d in range(1, xd):
+
+        @pl.when(x + d < xd)
+        def _(d=d):
+            px_copies[d - 1].start()
+
 
     def expand(value_ref, slot):
         for r in range(2):
@@ -379,19 +442,32 @@
         pltpu.make_async_remote_copy(vp.at[zd], xo.at[d - 1], xo_ss.at[d - 1], xo_rs.at[d - 1], device_id=at(dx=d), device_id_type=MESH)
         for d in range(1, xd)
     ]
-    for copy in xo_copies:
-        copy.start()
-    for copy in px_copies:
-        copy.wait()
+    for d in range(1, xd):
+
+        @pl.when(x + d < xd)
+        def _(d=d):
+            xo_copies[d - 1].start()
+
+    def settle(copies):
+        for d in range(1, xd):
+
+            @pl.when(x + d < xd)
+            def _(d=d):
+                copies[d - 1].wait_send()
+
+            @pl.when(x >= d)
+            def _(d=d):
+                copies[d - 1].wait_recv()
+
+    settle(px_copies)
 
     def expand_slot(d, carry):
         expand(px.at[d], d)
         return carry
 
-    lax.fori_loop(0, xd - 1, expand_slot, 0)
+    lax.fori_loop(0, x, expand_slot, 0)
     xp[0] = inflow_v[...]
-    for copy in xo_copies:
-        copy.wait()
+    settle(xo_copies)
 
     def x_step(i, carry):
         d = x - i - 1
@@ -445,7 +521,8 @@
                 pltpu.VMEM((NCLASS, 16, 16), F32),
                 pltpu.VMEM((4, NCLASS, 16, 16), F32),
                 pltpu.VMEM((2, 16, LANES), F32),
-                pltpu.VMEM((2, 2, 64, LANES), BF16),
+                pltpu.VMEM((2, 32, LANES), BF16),
+                pltpu.VMEM((2, 32, LANES), BF16),
                 pltpu.VMEM((16, LANES), F32),
                 pltpu.VMEM((16, LANES), F32),
                 pltpu.VMEM((NCLASS, 64, 64), BF16),
@@ -469,6 +546,8 @@
                 pltpu.VMEM((xd, 2, 16, LANES), F32),
                 pltpu.VMEM((2, 16, LANES), F32),
                 pltpu.VMEM((2, 16, LANES), F32),
+                pltpu.SemaphoreType.REGULAR((1,)),
+                pltpu.SemaphoreType.REGULAR((2,)),
                 dma((8,)),
                 dma((2,)),
                 dma((2,)),

time: 33.9 us -> 31.6 us (0.932)
  the two profiles are of different devices: /device:TPU:8 before, /device:TPU:6 now
where the time goes in v3:
time: 31.6 us; the launch traced here: 31.3 us
  Pallas kernels  30.6 us (97%)
  local copies, waits for them, and re-layouts  0.66 us (2%)
    pallas_call x1, Pallas kernels, on_device(): pl.pallas_call(functools.partial(kernel, xd, zd, yd), name='sweep', out_s...  30.6 us
    unnamed x1, local copies, waits for them, and re-layouts  0.66 us

profile of v3, /device:TPU:6, one launch (start us, length us, event | category | flops | bytes accessed | tf_op | source)
XLA Modules:
  0.0 31.3 jit_solution(97506134810760144)
XLA Ops:
  0.0 30.6 %sweep.1 = f32[2,2,64,128]{3,2,1,0:T(8,128)S(1)} custom-call(bf16[2,2,64,128]{3,2,1,0:T(8,128)(2,1)} %u_hbm.1, bf16[2,2,64,128]{3,2,1,0:T(8,128)(2,1)} %rhs_hbm.1, s32[2,2,16]{2,1,0:T(2,128)} %cls_hbm.1, s32[2,2,2,16]{3,2,1,0:T(2,128)} %flg_hbm.1, f32[8,64,64]{2,1,0:T(8,128)} %inv_hbm.1, f32[8,16,16]{2,1,0:T(8,128)} %xf_hbm.1, f32[4,8,16,16]{3,2,1,0:T(8,128)} %lat_hbm.1, ...), custom_call_target="tpu_custom_call" | custom-call | tf_op jit(solution)/shard_map/sweep/pallas_call | solution.py:509
  30.6 0.7 %copy.10 = f32[2,2,64,128]{3,2,1,0:T(8,128)} copy(f32[2,2,64,128]{3,2,1,0:T(8,128)S(1)} %sweep.1) | data formatting | bytes 262144

commit v4 on v3

--- a/solution.py
+++ b/solution.py
@@ -18,13 +18,11 @@
 
 def gather_plan(ring):
     assert ring == 16
-    far = (5, -5)
-    near = (2, -2, 1, -1)
-    own = [(0, step) for step in near]
-    relays = {5: [(5, 3)] + [(5, step) for step in near], 11: [(11, step) for step in near]}
-    covered = {0, 5, 11} | {(held + step) % ring for held, step in own + relays[5] + relays[11]}
+    own = (5, -5, 3, -3, 2, -2, 1, -1)
+    relays = {5: (2, 1, -1), 11: (-2, -1, 1)}
+    covered = {0, 8} | {step % ring for step in own} | {(held + step) % ring for held, steps in relays.items() for step in steps}
     assert covered == set(range(ring)), covered
-    return far, own, relays
+    return own, relays
 
 
 def iota(shape, axis):
@@ -81,7 +79,7 @@
     ]
     for load in loads:
         load.start()
-    far, own_near, relays = gather_plan(zd)
+    own_steps, relays = gather_plan(zd)
     barrier = pltpu.get_barrier_semaphore()
     for peer in (at(dy=1), at(dy=-1)) + tuple(at(dz=d) for d in (1, -1, 2, -2, 3, -3)):
         pl.semaphore_signal(barrier, inc=1, device_id=peer, device_id_type=MESH)
@@ -95,6 +93,9 @@
         pl.semaphore_signal(barrier, inc=1, device_id=at(dx=1), device_id_type=MESH)
 
     greeted = 8 + jnp.where(x > 0, 1, 0) + jnp.where(x < xd - 1, 1, 0)
+
+    def settle(semaphore, ref):
+        pltpu.make_async_copy(ref, ref, semaphore).wait()
 
     def tell(semaphore, step):
         for sign in (1, -1):
@@ -128,44 +129,41 @@
     border[1] = jnp.concatenate(packed_bottom, axis=0).astype(BF16)
     pl.semaphore_wait(barrier, greeted)
 
+    tell(know.at[0], 2)
+
     halo_copies = [
-        pltpu.make_async_remote_copy(border.at[0], halo.at[0], halo_ss.at[0], halo_rs.at[0], device_id=at(dy=1), device_id_type=MESH),
-        pltpu.make_async_remote_copy(border.at[1], halo.at[1], halo_ss.at[1], halo_rs.at[1], device_id=at(dy=-1), device_id_type=MESH),
+        pltpu.make_async_remote_copy(border.at[0], halo.at[0], halo_ss, halo_rs, device_id=at(dy=1), device_id_type=MESH),
+        pltpu.make_async_remote_copy(border.at[1], halo.at[1], halo_ss, halo_rs, device_id=at(dy=-1), device_id_type=MESH),
     ]
     for copy in halo_copies:
         copy.start()
-    tell(know.at[0], 2)
-
     @pl.when((x > 0) & (x < xd - 1))
     def _():
         pl.semaphore_signal(know_x.at[0], inc=1, device_id=at(dx=-1), device_id_type=MESH)
 
-    def sender(buffer, send_sems, recv_sems):
-        copies = {}
-
-        def send(held, step):
-            to = (held + step) % zd
-            copies[to] = pltpu.make_async_remote_copy(buffer.at[held], buffer.at[to], send_sems.at[to - 1], recv_sems.at[to - 1], device_id=at(dz=step), device_id_type=MESH)
-            copies[to].start()
-
-        return copies, send
-
-    cls_copies, send_cls = sender(clsb, cls_ss, cls_rs)
-    o_copies, send_o = sender(ob, o_ss, o_rs)
-
-    def send_own(send):
-        for step in far:
-            send(0, step)
-        for held, step in own_near:
-            send(held, step)
-
-    for held, step in own_near:
-        send_cls(held, step)
-
-    def relay(copies, send, offset):
-        copies[offset].wait_recv()
-        for held, step in relays[offset]:
-            send(held, step)
+    near_steps = (3, 2, -2, 1, -1)
+    filled = {"cls": [], "o": []}
+
+    def send_cls(held, step):
+        to = (held + step) % zd
+        assert to not in filled["cls"]
+        filled["cls"].append(to)
+        arrival = cls_rs.at[0 if held == 0 and step in near_steps else 1]
+        pltpu.make_async_remote_copy(clsb.at[held], clsb.at[to], cls_ss, arrival, device_id=at(dz=step), device_id_type=MESH).start()
+
+    def send_o(held, step):
+        to = (held + step) % zd
+        assert to not in filled["o"]
+        filled["o"].append(to)
+        arrival = o_rs.at[0 if to == 5 else 1 if to == 11 else 2]
+        pltpu.make_async_remote_copy(ob.at[held], ob.at[to], o_ss, arrival, device_id=at(dz=step), device_id_type=MESH).start()
+
+    for step in near_steps:
+        send_cls(0, step)
+    halves_of_8 = [
+        pltpu.make_async_remote_copy(ob.at[held, r], ob.at[8, r], o_ss, o_rs.at[2], device_id=at(dz=step), device_id_type=MESH)
+        for r, (held, step) in enumerate([(5, 3), (11, -3)])
+    ]
 
     loads[3].wait()
     loads[4].wait()
@@ -228,15 +226,15 @@
             src[p, pl.ds(32, 64), columns] = z_source.astype(BF16)
             src[p, pl.ds(96, 32), columns] = jnp.zeros((32, LANES), BF16)
 
-    for d in (1, 2, zd - 1, zd - 2):
-        cls_copies[d].wait_recv()
-    pl.semaphore_wait(know.at[0], 2)
-    for held in (0, 1, zd - 1, 2, zd - 2):
-        for step in far:
-            send_cls(held, step)
-
-    for copy in halo_copies:
-        copy.wait()
+    settle(halo_rs, halo)
+
+    @pl.when(x < xd - 2)
+    def _():
+        pl.semaphore_wait(know_x.at[0], 1)
+
+    @pl.when((x > 0) & (x < xd - 2))
+    def _():
+        pl.semaphore_signal(know_x.at[1], inc=1, device_id=at(dx=-1), device_id_type=MESH)
 
     has_below = jnp.where(gy > 0, 1.0, 0.0)
     has_above = jnp.where(gy < yd - 1, 1.0, 0.0)
@@ -295,7 +293,11 @@
         for half in range(2):
             ob[0, r, halves[half], :] = parts[half] + wo[1, r, halves[half], :]
 
-    send_own(send_o)
+    pl.semaphore_wait(know.at[0], 2)
+    for step in own_steps[:2]:
+        send_o(0, step)
+    for step in (5, -5):
+        send_cls(0, step)
 
     lane8 = iota((8, LANES), 1)
     pair_first, pair_second = ((lane8 >> 3) & 7) * 16, (lane8 & 7) * 16
@@ -322,18 +324,12 @@
 
     lax.fori_loop(0, 16, pair_product, 0)
 
-    @pl.when(x < xd - 2)
-    def _():
-        pl.semaphore_wait(know_x.at[0], 1)
-
-    @pl.when((x > 0) & (x < xd - 2))
-    def _():
-        pl.semaphore_signal(know_x.at[1], inc=1, device_id=at(dx=-1), device_id_type=MESH)
-
-    @pl.when(x < xd - 3)
-    def _():
-        pl.semaphore_wait(know_x.at[1], 1)
-
+    settle(cls_rs.at[0], clsb.at[pl.ds(0, 5)])
+    for held in (2, zd - 2, 1, zd - 1):
+        for step in (5, -5):
+            if (held + step) % zd not in filled["cls"]:
+                send_cls(held, step)
+    send_cls(3, 5)
     def full_planes(p, carry):
         source = src[p]
         both = jnp.concatenate([source, source], axis=0)
@@ -363,17 +359,18 @@
             for r in range(2):
                 ec[d, r] = every[:, r * LANES : (r + 1) * LANES].reshape(16, 16, LANES)
 
+    for step in own_steps[2:]:
+        send_o(0, step)
+    assert len(filled["cls"]) == zd - 1
     propagators((0, 1, 15, 2, 14))
-    middle = (7, 3, 13, 5, 11, 4, 12, 6, 10, 9)
-    for d in middle:
-        cls_copies[d].wait_recv()
-        if d == 7:
-            send_cls(7, 1)
-    for offset in relays:
-        relay(o_copies, send_o, offset)
+    for r, (held, steps) in enumerate(relays.items()):
+        settle(o_rs.at[r], ob.at[held])
+        halves_of_8[r].start()
+        for step in steps:
+            send_o(held, step)
+    middle = (3, 5, 11, 4, 12, 6, 10, 7, 9, 13, 8)
+    settle(cls_rs.at[1], clsb.at[pl.ds(0, zd - 6)])
     propagators(middle)
-    cls_copies[8].wait_recv()
-    propagators((8,))
 
     def unit_step(i, carry):
         d = lax.rem(z - i + zd, zd)
@@ -395,8 +392,12 @@
             up[0, r, h] = (iota((16, LANES), 0) == (lane16 >> 4) + 8 * h).astype(F32)
     lax.fori_loop(0, zd, unit_step, 0)
 
+    @pl.when(x < xd - 3)
+    def _():
+        pl.semaphore_wait(know_x.at[1], 1)
+
     px_copies = [
-        pltpu.make_async_remote_copy(up.at[zd], px.at[d - 1], px_ss.at[d - 1], px_rs.at[d - 1], device_id=at(dx=d), device_id_type=MESH)
+        pltpu.make_async_remote_copy(up.at[zd], px.at[d - 1], px_ss, px_rs, device_id=at(dx=d), device_id_type=MESH)
         for d in range(1, xd)
     ]
     for d in range(1, xd):
@@ -424,9 +425,8 @@
                 sums[half].append(factors[m, halves[half], :] * value)
         return total_of(sums[0]), total_of(sums[1])
 
-    for d in range(1, zd):
-        if d not in relays:
-            o_copies[d].wait_recv()
+    assert len(filled["o"]) == zd - 2
+    settle(o_rs.at[2], ob.at[pl.ds(0, zd - 3)])
     vp[0] = jnp.zeros((2, 16, LANES), F32)
 
     def group_step(i, carry):
@@ -439,7 +439,7 @@
 
     lax.fori_loop(0, zd, group_step, 0)
     xo_copies = [
-        pltpu.make_async_remote_copy(vp.at[zd], xo.at[d - 1], xo_ss.at[d - 1], xo_rs.at[d - 1], device_id=at(dx=d), device_id_type=MESH)
+        pltpu.make_async_remote_copy(vp.at[zd], xo.at[d - 1], xo_ss, xo_rs, device_id=at(dx=d), device_id_type=MESH)
         for d in range(1, xd)
     ]
     for d in range(1, xd):
@@ -448,18 +448,18 @@
         def _(d=d):
             xo_copies[d - 1].start()
 
-    def settle(copies):
-        for d in range(1, xd):
-
-            @pl.when(x + d < xd)
-            def _(d=d):
-                copies[d - 1].wait_send()
-
-            @pl.when(x >= d)
-            def _(d=d):
-                copies[d - 1].wait_recv()
-
-    settle(px_copies)
+    def settle_x(send_sem, recv_sem, ref):
+        for n in range(1, xd):
+
+            @pl.when(x == xd - 1 - n)
+            def _(n=n):
+                settle(send_sem, ref.at[pl.ds(0, n)])
+
+            @pl.when(x == n)
+            def _(n=n):
+                settle(recv_sem, ref.at[pl.ds(0, n)])
+
+    settle_x(px_ss, px_rs, px)
 
     def expand_slot(d, carry):
         expand(px.at[d], d)
@@ -467,7 +467,7 @@
 
     lax.fori_loop(0, x, expand_slot, 0)
     xp[0] = inflow_v[...]
-    settle(xo_copies)
+    settle_x(xo_ss, xo_rs, xo)
 
     def x_step(i, carry):
         d = x - i - 1
@@ -494,8 +494,9 @@
         for r in range(2):
             out_ref[p, r] = out_ref[p, r] + pick_class(stacked[:, r * LANES : (r + 1) * LANES], 64, class_masks(p, r, 64))
 
-    for copy in list(cls_copies.values()) + list(o_copies.values()):
-        copy.wait_send()
+    settle(halo_ss, halo)
+    settle(cls_ss, clsb.at[pl.ds(0, zd - 1)])
+    settle(o_ss, ob.at[pl.ds(0, zd - 1)])
 
 
 def solution(mesh):
@@ -549,16 +550,16 @@
                 pltpu.SemaphoreType.REGULAR((1,)),
                 pltpu.SemaphoreType.REGULAR((2,)),
                 dma((8,)),
+                dma,
+                dma,
+                dma,
                 dma((2,)),
-                dma((2,)),
-                dma((zd - 1,)),
-                dma((zd - 1,)),
-                dma((zd - 1,)),
-                dma((zd - 1,)),
-                dma((xd - 1,)),
-                dma((xd - 1,)),
-                dma((xd - 1,)),
-                dma((xd - 1,)),
+                dma,
+                dma((3,)),
+                dma,
+                dma,
+                dma,
+                dma,
             ],
             compiler_params=pltpu.CompilerParams(collective_id=0, has_side_effects=True),
         )(u_old, rhs, classes, flags, inverse, x_face, lateral_faces, inflow)

time: 31.6 us -> 29.9 us (0.946)
  Pallas kernels: 30.6 us -> 29.1 us
    pallas_call x1, Pallas kernels: 30.6 us -> 29.1 us  [on_device(): pl.pallas_call(functools.partial(kernel, xd, zd, yd), name='sweep', out_s...]
where the time goes in v4:
time: 29.9 us; the launch traced here: 29.7 us
  Pallas kernels  29.1 us (97%)
  local copies, waits for them, and re-layouts  0.66 us (2%)
    pallas_call x1, Pallas kernels, on_device(): pl.pallas_call(functools.partial(kernel, xd, zd, yd), name='sweep', out_s...  29.1 us
    unnamed x1, local copies, waits for them, and re-layouts  0.66 us

profile of v4, /device:TPU:6, one launch (start us, length us, event | category | flops | bytes accessed | tf_op | source)
XLA Modules:
  0.0 29.7 jit_solution(13095666705519342943)
XLA Ops:
  0.0 29.1 %sweep.1 = f32[2,2,64,128]{3,2,1,0:T(8,128)S(1)} custom-call(bf16[2,2,64,128]{3,2,1,0:T(8,128)(2,1)} %u_hbm.1, bf16[2,2,64,128]{3,2,1,0:T(8,128)(2,1)} %rhs_hbm.1, s32[2,2,16]{2,1,0:T(2,128)} %cls_hbm.1, s32[2,2,2,16]{3,2,1,0:T(2,128)} %flg_hbm.1, f32[8,64,64]{2,1,0:T(8,128)} %inv_hbm.1, f32[8,16,16]{2,1,0:T(8,128)} %xf_hbm.1, f32[4,8,16,16]{3,2,1,0:T(8,128)} %lat_hbm.1, ...), custom_call_target="tpu_custom_call" | custom-call | tf_op jit(solution)/shard_map/sweep/pallas_call | solution.py:510
  29.1 0.7 %copy.10 = f32[2,2,64,128]{3,2,1,0:T(8,128)} copy(f32[2,2,64,128]{3,2,1,0:T(8,128)S(1)} %sweep.1) | data formatting | bytes 262144

commit v5 on v4

--- a/solution.py
+++ b/solution.py
@@ -71,6 +71,29 @@
         gx_to = lax.rem(x + dx + xd, xd) * zd + lax.rem(z + dz + zd, zd)
         return (gx_to, lax.rem(gy + dy + yd, yd))
 
+    own_steps, relays = gather_plan(zd)
+    barrier = pltpu.get_barrier_semaphore()
+    for d in (3, -3, 2, -2, 1, -1):
+        pl.semaphore_signal(barrier, inc=1, device_id=at(dz=d), device_id_type=MESH)
+    has_below, has_above = gy > 0, gy < yd - 1
+
+    @pl.when(has_above)
+    def _():
+        pl.semaphore_signal(barrier, inc=1, device_id=at(dy=1), device_id_type=MESH)
+
+    @pl.when(has_below)
+    def _():
+        pl.semaphore_signal(barrier, inc=1, device_id=at(dy=-1), device_id_type=MESH)
+
+    @pl.when(x > 0)
+    def _():
+        pl.semaphore_signal(barrier, inc=1, device_id=at(dx=-1), device_id_type=MESH)
+
+    @pl.when(x < xd - 1)
+    def _():
+        pl.semaphore_signal(barrier, inc=1, device_id=at(dx=1), device_id_type=MESH)
+
+    greeted = 6 + sum(jnp.where(there, 1, 0) for there in (has_below, has_above, x > 0, x < xd - 1))
     loads = [
         pltpu.make_async_copy(a, b, local_sem.at[i])
         for i, (a, b) in enumerate(
@@ -79,20 +102,6 @@
     ]
     for load in loads:
         load.start()
-    own_steps, relays = gather_plan(zd)
-    barrier = pltpu.get_barrier_semaphore()
-    for peer in (at(dy=1), at(dy=-1)) + tuple(at(dz=d) for d in (1, -1, 2, -2, 3, -3)):
-        pl.semaphore_signal(barrier, inc=1, device_id=peer, device_id_type=MESH)
-
-    @pl.when(x > 0)
-    def _():
-        pl.semaphore_signal(barrier, inc=1, device_id=at(dx=-1), device_id_type=MESH)
-
-    @pl.when(x < xd - 1)
-    def _():
-        pl.semaphore_signal(barrier, inc=1, device_id=at(dx=1), device_id_type=MESH)
-
-    greeted = 8 + jnp.where(x > 0, 1, 0) + jnp.where(x < xd - 1, 1, 0)
 
     def settle(semaphore, ref):
         pltpu.make_async_copy(ref, ref, semaphore).wait()
@@ -135,20 +144,34 @@
         pltpu.make_async_remote_copy(border.at[0], halo.at[0], halo_ss, halo_rs, device_id=at(dy=1), device_id_type=MESH),
         pltpu.make_async_remote_copy(border.at[1], halo.at[1], halo_ss, halo_rs, device_id=at(dy=-1), device_id_type=MESH),
     ]
-    for copy in halo_copies:
-        copy.start()
+    @pl.when(has_above)
+    def _():
+        halo_copies[0].start()
+
+    @pl.when(has_below)
+    def _():
+        halo_copies[1].start()
+
+    @pl.when(gy == 0)
+    def _():
+        halo[0] = jnp.zeros((32, LANES), BF16)
+
+    @pl.when(gy == yd - 1)
+    def _():
+        halo[1] = jnp.zeros((32, LANES), BF16)
+
     @pl.when((x > 0) & (x < xd - 1))
     def _():
         pl.semaphore_signal(know_x.at[0], inc=1, device_id=at(dx=-1), device_id_type=MESH)
 
-    near_steps = (3, 2, -2, 1, -1)
+    near_steps = (2, -2, 3, 1, -1)
     filled = {"cls": [], "o": []}
 
     def send_cls(held, step):
         to = (held + step) % zd
         assert to not in filled["cls"]
         filled["cls"].append(to)
-        arrival = cls_rs.at[0 if held == 0 and step in near_steps else 1]
+        arrival = cls_rs.at[{3: 2, 8: 3}.get(to, 0 if held == 0 and step in near_steps else 1)]
         pltpu.make_async_remote_copy(clsb.at[held], clsb.at[to], cls_ss, arrival, device_id=at(dz=step), device_id_type=MESH).start()
 
     def send_o(held, step):
@@ -226,7 +249,16 @@
             src[p, pl.ds(32, 64), columns] = z_source.astype(BF16)
             src[p, pl.ds(96, 32), columns] = jnp.zeros((32, LANES), BF16)
 
-    settle(halo_rs, halo)
+    def settle_y(semaphore):
+        @pl.when(has_below & has_above)
+        def _():
+            settle(semaphore, halo)
+
+        @pl.when(jnp.logical_not(has_below & has_above))
+        def _():
+            settle(semaphore, halo.at[0])
+
+    settle_y(halo_rs)
 
     @pl.when(x < xd - 2)
     def _():
@@ -236,18 +268,14 @@
     def _():
         pl.semaphore_signal(know_x.at[1], inc=1, device_id=at(dx=-1), device_id_type=MESH)
 
-    has_below = jnp.where(gy > 0, 1.0, 0.0)
-    has_above = jnp.where(gy < yd - 1, 1.0, 0.0)
     got_below, got_above = halo[0].astype(F32), halo[1].astype(F32)
     for p in range(2):
         for r in range(2):
             y_flag = meta[pl.ds(4 + p * 2 + r, 1), :]
             m_below, m_above = 1.0 - y_flag, y_flag
             if r == 0:
-                m_below = m_below * has_below
                 other = u_v[p, 1].astype(F32)
             else:
-                m_above = m_above * has_above
                 other = u_v[p, 0].astype(F32)
             pieces = []
             for a_ in range(4):
@@ -324,12 +352,11 @@
 
     lax.fori_loop(0, 16, pair_product, 0)
 
-    settle(cls_rs.at[0], clsb.at[pl.ds(0, 5)])
+    settle(cls_rs.at[0], clsb.at[pl.ds(0, 4)])
     for held in (2, zd - 2, 1, zd - 1):
         for step in (5, -5):
             if (held + step) % zd not in filled["cls"]:
                 send_cls(held, step)
-    send_cls(3, 5)
     def full_planes(p, carry):
         source = src[p]
         both = jnp.concatenate([source, source], axis=0)
@@ -359,6 +386,8 @@
             for r in range(2):
                 ec[d, r] = every[:, r * LANES : (r + 1) * LANES].reshape(16, 16, LANES)
 
+    settle(cls_rs.at[2], clsb.at[3])
+    send_cls(3, 5)
     for step in own_steps[2:]:
         send_o(0, step)
     assert len(filled["cls"]) == zd - 1
@@ -368,9 +397,11 @@
         halves_of_8[r].start()
         for step in steps:
             send_o(held, step)
-    middle = (3, 5, 11, 4, 12, 6, 10, 7, 9, 13, 8)
-    settle(cls_rs.at[1], clsb.at[pl.ds(0, zd - 6)])
+    middle = (3, 5, 11, 4, 12, 6, 10, 7, 9, 13)
+    settle(cls_rs.at[1], clsb.at[pl.ds(0, len(middle) - 1)])
     propagators(middle)
+    settle(cls_rs.at[3], clsb.at[8])
+    propagators((8,))
 
     def unit_step(i, carry):
         d = lax.rem(z - i + zd, zd)
@@ -415,7 +446,6 @@
                     for unit in range(8):
                         ex[slot, r, 8 * h + unit, halves[half], :] = lanes_of(whole, lane_low + 16 * unit)
 
-    expand(up.at[z], xd - 1)
 
     def apply(factors, source):
         sums = [[], []]
@@ -448,6 +478,7 @@
         def _(d=d):
             xo_copies[d - 1].start()
 
+    expand(up.at[z], xd - 1)
     def settle_x(send_sem, recv_sem, ref):
         for n in range(1, xd):
 
@@ -494,7 +525,7 @@
         for r in range(2):
             out_ref[p, r] = out_ref[p, r] + pick_class(stacked[:, r * LANES : (r + 1) * LANES], 64, class_masks(p, r, 64))
 
-    settle(halo_ss, halo)
+    settle_y(halo_ss)
     settle(cls_ss, clsb.at[pl.ds(0, zd - 1)])
     settle(o_ss, ob.at[pl.ds(0, zd - 1)])
 
@@ -553,7 +584,7 @@
                 dma,
                 dma,
                 dma,
-                dma((2,)),
+                dma((4,)),
                 dma,
                 dma((3,)),
                 dma,

time: 29.9 us -> 28.9 us (0.967)
  Pallas kernels: 29.1 us -> 28 us
    pallas_call x1, Pallas kernels: 29.1 us -> 28 us  [on_device(): pl.pallas_call(functools.partial(kernel, xd, zd, yd), name='sweep', out_s...]
where the time goes in v5:
time: 28.9 us; the launch traced here: 28.7 us
  Pallas kernels  28 us (97%)
  local copies, waits for them, and re-layouts  0.66 us (2%)
    pallas_call x1, Pallas kernels, on_device(): pl.pallas_call(functools.partial(kernel, xd, zd, yd), name='sweep', out_s...  28 us
    unnamed x1, local copies, waits for them, and re-layouts  0.66 us

profile of v5, /device:TPU:6, one launch (start us, length us, event | category | flops | bytes accessed | tf_op | source)
XLA Modules:
  0.0 28.7 jit_solution(13817236370364850995)
XLA Ops:
  0.0 28.0 %sweep.1 = f32[2,2,64,128]{3,2,1,0:T(8,128)S(1)} custom-call(bf16[2,2,64,128]{3,2,1,0:T(8,128)(2,1)} %u_hbm.1, bf16[2,2,64,128]{3,2,1,0:T(8,128)(2,1)} %rhs_hbm.1, s32[2,2,16]{2,1,0:T(2,128)} %cls_hbm.1, s32[2,2,2,16]{3,2,1,0:T(2,128)} %flg_hbm.1, f32[8,64,64]{2,1,0:T(8,128)} %inv_hbm.1, f32[8,16,16]{2,1,0:T(8,128)} %xf_hbm.1, f32[4,8,16,16]{3,2,1,0:T(8,128)} %lat_hbm.1, ...), custom_call_target="tpu_custom_call" | custom-call | tf_op jit(solution)/shard_map/sweep/pallas_call | solution.py:541
  28.0 0.7 %copy.10 = f32[2,2,64,128]{3,2,1,0:T(8,128)} copy(f32[2,2,64,128]{3,2,1,0:T(8,128)S(1)} %sweep.1) | data formatting | bytes 262144

commit v6 on v5

--- a/solution.py
+++ b/solution.py
@@ -61,7 +61,7 @@
     out_ref,
     u_v, rhs_v, cls_v, flg_v, inv_v, xf_v, lat_v, inflow_v, border, halo,
     meta_in, meta, ih, il, mhl, tw, c1s, t0s, pairs, src, rh, wo,
-    clsb, ob, ec, up, vp, px, xo, ex, xp, ent, tr1,
+    clsb, ob, ec, own, up, vp, px, xo, ex, xp, ent, tr1,
     know, know_x, local_sem, halo_ss, halo_rs, cls_ss, cls_rs, o_ss, o_rs, px_ss, px_rs, xo_ss, xo_rs,
 ):
     gx, gy = lax.axis_index("gx"), lax.axis_index("gy")
@@ -232,6 +232,13 @@
     tw[...] = tw_value
     halves = [pl.ds(0, 8), pl.ds(8, 8)]
 
+    for p in range(2):
+        for r in range(2):
+            base = (jnp.broadcast_to(meta[pl.ds(p * 2 + r, 1), :], (8, LANES)) * 16.0).astype(jnp.int32)
+            for m in range(16):
+                for half in range(2):
+                    own[p, r, m, halves[half], :] = lanes_of(tw_value[half * 8 : half * 8 + 8], base + m)
+
     loads[6].wait()
     loads[7].wait()
     lane64, node64 = iota((64, LANES), 1), iota((64, LANES), 0)
@@ -241,10 +248,10 @@
         for r in range(2):
             columns = pl.ds(r * LANES, LANES)
             rh[p, :, columns] = rhs_v[p, r]
-            own = u_v[p, r].astype(F32)
+            here = u_v[p, r].astype(F32)
             z_flag = meta[pl.ds(8 + p * 2 + r, 1), :]
-            front = jnp.where(lane_z > 0, pltpu.roll(own, 1, 1), 0.0) * (1.0 - z_flag)
-            back = jnp.where(lane_z < 15, pltpu.roll(own, LANES - 1, 1), 0.0) * z_flag
+            front = jnp.where(lane_z > 0, pltpu.roll(here, 1, 1), 0.0) * (1.0 - z_flag)
+            back = jnp.where(lane_z < 15, pltpu.roll(here, LANES - 1, 1), 0.0) * z_flag
             z_source = jnp.where(node_c == 3, front, jnp.where(node_c == 0, back, 0.0))
             src[p, pl.ds(32, 64), columns] = z_source.astype(BF16)
             src[p, pl.ds(96, 32), columns] = jnp.zeros((32, LANES), BF16)
@@ -307,17 +314,16 @@
         for r in range(2):
             wo[p, r] = pick_class(stacked[:, r * LANES : (r + 1) * LANES], 16, class_masks(p, r, 16))
 
-    def class_step(index_row, source_ref):
-        base = (jnp.broadcast_to(meta[pl.ds(index_row, 1), :], (8, LANES)) * 16.0).astype(jnp.int32)
+    def apply(factors, source):
         sums = [[], []]
         for m in range(16):
-            value = spread(source_ref, m)
+            value = spread(source, m)
             for half in range(2):
-                sums[half].append(lanes_of(tw[halves[half], :], base + m) * value)
+                sums[half].append(factors[m, halves[half], :] * value)
         return total_of(sums[0]), total_of(sums[1])
 
     for r in range(2):
-        parts = class_step(2 + r, wo.at[0, r])
+        parts = apply(own.at[1, r], wo.at[0, r])
         for half in range(2):
             ob[0, r, halves[half], :] = parts[half] + wo[1, r, halves[half], :]
 
@@ -388,10 +394,12 @@
 
     settle(cls_rs.at[2], clsb.at[3])
     send_cls(3, 5)
-    for step in own_steps[2:]:
+    for step in own_steps[2:4]:
         send_o(0, step)
     assert len(filled["cls"]) == zd - 1
     propagators((0, 1, 15, 2, 14))
+    for step in own_steps[4:]:
+        send_o(0, step)
     for r, (held, steps) in enumerate(relays.items()):
         settle(o_rs.at[r], ob.at[held])
         halves_of_8[r].start()
@@ -447,14 +455,6 @@
                         ex[slot, r, 8 * h + unit, halves[half], :] = lanes_of(whole, lane_low + 16 * unit)
 
 
-    def apply(factors, source):
-        sums = [[], []]
-        for m in range(16):
-            value = spread(source, m)
-            for half in range(2):
-                sums[half].append(factors[m, halves[half], :] * value)
-        return total_of(sums[0]), total_of(sums[1])
-
     assert len(filled["o"]) == zd - 2
     settle(o_rs.at[2], ob.at[pl.ds(0, zd - 3)])
     vp[0] = jnp.zeros((2, 16, LANES), F32)
@@ -514,7 +514,7 @@
         for half in range(2):
             ent[r, halves[half], :] = parts[half] + vp[z, r, halves[half], :]
     for r in range(2):
-        parts = class_step(r, ent.at[r])
+        parts = apply(own.at[0, r], ent.at[r])
         for half in range(2):
             tr1[r, halves[half], :] = parts[half] + wo[0, r, halves[half], :]
 
@@ -570,6 +570,7 @@
                 pltpu.VMEM((zd, 1, LANES), F32),
                 pltpu.VMEM((zd, 2, 16, LANES), F32),
                 pltpu.VMEM((zd, 2, 16, 16, LANES), F32),
+                pltpu.VMEM((2, 2, 16, 16, LANES), F32),
                 pltpu.VMEM((zd + 1, 2, 2, 16, LANES), F32),
                 pltpu.VMEM((zd + 1, 2, 16, LANES), F32),
                 pltpu.VMEM((xd - 1, 2, 2, 16, LANES), F32),

time: 28.9 us -> 28.6 us (0.990)
  no operation moved by 1% of the time
where the time goes in v6:
time: 28.6 us; the launch traced here: 28.5 us
  Pallas kernels  27.8 us (97%)
  local copies, waits for them, and re-layouts  0.66 us (2%)
    pallas_call x1, Pallas kernels, on_device(): pl.pallas_call(functools.partial(kernel, xd, zd, yd), name='sweep', out_s...  27.8 us
    unnamed x1, local copies, waits for them, and re-layouts  0.66 us

profile of v6, /device:TPU:6, one launch (start us, length us, event | category | flops | bytes accessed | tf_op | source)
XLA Modules:
  0.0 28.5 jit_solution(15410036251510568318)
XLA Ops:
  0.0 27.8 %sweep.1 = f32[2,2,64,128]{3,2,1,0:T(8,128)S(1)} custom-call(bf16[2,2,64,128]{3,2,1,0:T(8,128)(2,1)} %u_hbm.1, bf16[2,2,64,128]{3,2,1,0:T(8,128)(2,1)} %rhs_hbm.1, s32[2,2,16]{2,1,0:T(2,128)} %cls_hbm.1, s32[2,2,2,16]{3,2,1,0:T(2,128)} %flg_hbm.1, f32[8,64,64]{2,1,0:T(8,128)} %inv_hbm.1, f32[8,16,16]{2,1,0:T(8,128)} %xf_hbm.1, f32[4,8,16,16]{3,2,1,0:T(8,128)} %lat_hbm.1, ...), custom_call_target="tpu_custom_call" | custom-call | tf_op jit(solution)/shard_map/sweep/pallas_call | solution.py:541
  27.8 0.7 %copy.10 = f32[2,2,64,128]{3,2,1,0:T(8,128)} copy(f32[2,2,64,128]{3,2,1,0:T(8,128)S(1)} %sweep.1) | data formatting | bytes 262144
